TPU v7x, 256 devices: a whole 4x4x8 slice. The times are simulated.
256 devices in a mesh: grp: 32 (over z_lo, x, core), shard: 8 (over z_hi, y).
Axes of the slice: x: 4, y: 4, z: 8 (z_hi: 2, z_lo: 4; z = z_hi * 4 + z_lo), core: 2. Of those that a mesh axis runs over, the one named last changes fastest.
Arguments:
- tokens: bfloat16 [16384, 2560], P(('grp', 'shard')), may hold values from -0.125 to 0.125
- target: bfloat16 [16384, 13824], P('grp', 'shard'), may hold values from -6 to 6
- post_mean: float32 [2560, 13824], P('grp', 'shard'), may hold values from -5 to 5
- post_hess: float32 [2560, 13824], P('grp', 'shard'), may hold values from 0.05 to 0.5
- weight_noise: bfloat16 [32, 2560, 13824], P(None, 'grp', 'shard'), may hold values from -6 to 6
Outputs:
- new_mean: float32 [2560, 13824], P('grp', 'shard')
- new_hess: float32 [2560, 13824], P('grp', 'shard')
All inputs are finite; a program needn't handle non-finite values.
Results may differ from a plain program's by a relative error of at most 0.0018.
Values may be sent and summed in bfloat16 or wider, within the bound.
A program may use at most 192 MiB of HBM per device.

v0:
```python
import jax
import jax.numpy as jnp
from jax import lax
from jax.sharding import PartitionSpec as P

sample_size = 50.0
weight_decay = 0.02
hess_decay = 0.95
learn_rate = 0.3


def contract_rows(left, right):
    return lax.dot_general(
        left, right, (((0,), (0,)), ((), ())), preferred_element_type=jnp.float32
    )


def local(tokens, target, post_mean, post_hess, weight_noise):
    groups = weight_noise.shape[0]
    post_std = lax.rsqrt(sample_size * (post_hess + weight_decay))
    noise_vals = weight_noise.astype(jnp.float32)
    samples = (post_mean[None] + post_std[None] * noise_vals).astype(jnp.bfloat16)
    group_x = lax.all_gather(tokens, "shard", axis=0, tiled=True)
    output = jnp.dot(
        group_x,
        lax.all_to_all(samples, "grp", split_axis=0, concat_axis=1, tiled=True)[0],
        preferred_element_type=jnp.float32,
    )
    residual = (output - target.astype(jnp.float32)).astype(jnp.bfloat16)
    gradient = contract_rows(group_x, residual).astype(jnp.bfloat16)
    group_grads = lax.all_to_all(gradient[None], "grp", split_axis=1, concat_axis=0, tiled=True)
    group_grads = group_grads.astype(jnp.float32)
    mean_grad = jnp.sum(group_grads, axis=0) / groups
    hess_est = jnp.sum(group_grads * noise_vals, axis=0) / groups / post_std
    keep_rate = 1.0 - hess_decay
    gap = post_hess - hess_est
    new_hess = (
        hess_decay * post_hess
        + keep_rate * hess_est
        + 0.5 * keep_rate * keep_rate * gap * gap / (post_hess + weight_decay)
    )
    new_mean = post_mean - learn_rate * (mean_grad + weight_decay * post_mean) / (
        new_hess + weight_decay
    )
    return (new_mean, new_hess)


def solution(mesh):
    return jax.shard_map(
        local,
        mesh=mesh,
        in_specs=(
            P(("grp", "shard"), None),
            P("grp", "shard"),
            P("grp", "shard"),
            P("grp", "shard"),
            P(None, "grp", "shard"),
        ),
        out_specs=(P("grp", "shard"), P("grp", "shard")),
        check_vma=False,
    )
```

profile of v0, /device:TPU:1, one launch (start us, length us, event | category | flops | bytes accessed | tf_op | source)
XLA Modules:
  0.0 707.4 jit_solution(3777936069902256427)
XLA Ops:
  7.2 1.1 multiply_rsqrt_fusion
  8.3 9.5 %fusion.1 = bf16[32,80,1728]{2,1,0:T(8,128)(2,1)} fusion(bf16[32,80,1728]{2,1,0:T(8,128)(2,1)} %param.9, f32[80,1728]{1,0:T(8,128)S(1)} %multiply_rsqrt_fusion, f32[80,1728]{1,0:T(8,128)} %param.7), kind=kLoop, calls=%fused_computation.4 | loop fusion | flops 17694720 | bytes 18800640 | tf_op jit(solution)/shard_map/convert_element_type | solution.py:22
  17.8 0.0 copy-start.2
  17.8 10.2 %all-to-all-start = ((bf16[32,80,1728]{2,1,0:T(8,128)(2,1)}), bf16[32,80,1728]{2,1,0:T(8,128)(2,1)}, u32[]{:S(2)}, u32[]{:S(2)}) async-start(bf16[32,80,1728]{2,1,0:T(8,128)(2,1)} %fusion.1), calls=%async_computation | async-start | bytes 18350080 | tf_op jit(solution)/shard_map/all_to_all | solution.py:26
  28.0 0.2 all-gather.2.cloned.1.call-start
  28.2 0.5 all-gather.2.cloned.1.call-update
  28.7 108.1 %all-gather.2.cloned.1.call-done = bf16[512,2560]{1,0:T(8,128)(2,1)} async-done(((bf16[64,2560]{1,0:T(8,128)(2,1)}), bf16[512,2560]{1,0:T(8,128)(2,1)}) %all-gather.2.cloned.1.call-update) | async-done | bytes 2621456 | tf_op jit(solution)/shard_map/all_gather | solution.py:23
  136.9 129.7 %all-to-all-done = bf16[32,80,1728]{2,1,0:T(8,128)(2,1)} async-done(((bf16[32,80,1728]{2,1,0:T(8,128)(2,1)}), bf16[32,80,1728]{2,1,0:T(8,128)(2,1)}, u32[]{:S(2)}, u32[]{:S(2)}) %all-to-all-start) | async-done | bytes 8847392 | tf_op jit(solution)/shard_map/all_to_all | solution.py:26
  266.5 0.0 copy-done.2
  266.5 17.0 %fusion.3 = bf16[1,2560,1728]{1,2,0:T(8,128)(2,1)} fusion(bf16[512,2560]{1,0:T(8,128)(2,1)} %all-gather.2.cloned.1.call-done, bf16[512,1728]{0,1:T(8,128)(2,1)S(1)} %copy-done.2, bf16[2560,1728]{1,0:T(8,128)(2,1)} %bitcast), kind=kOutput, calls=%fused_computation.7 | convolution fusion | flops 9066774528 | bytes 22085632 | tf_op jit(solution)/shard_map/dot_general | solution.py:13
  283.6 37.2 %copy.9 = bf16[1,2560,1728]{2,0,1:T(2,128)(2,1)} copy(bf16[1,2560,1728]{1,2,0:T(8,128)(2,1)} %fusion.3) | data formatting | bytes 17694720 | tf_op jit(solution)/shard_map/broadcast_in_dim | solution.py:31
  320.7 0.5 broadcast.21
  321.2 101.7 %reduce = bf16[2560,1728]{1,0:T(8,128)(2,1)} reduce(bf16[2560,1,1728]{2,1,0:T(2,128)(2,1)} %bitcast.18, bf16[]{:T(256)} %broadcast.21), dimensions={1}, to_apply=%bitcast.13.reduce_sub_computation | reduce | bytes 17694722
  422.9 24.1 %reshape.16 = bf16[32,2,69120]{2,1,0:T(2,128)(2,1)} reshape(bf16[2560,1728]{1,0:T(8,128)(2,1)} %reduce) | data formatting | bytes 17694720
  447.0 200.5 %all_to_all.8 = bf16[32,2,69120]{2,1,0:T(2,128)(2,1)} all-to-all(bf16[32,2,69120]{2,1,0:T(2,128)(2,1)} %reshape.16), channel_id=1, replica_groups=mesh['grp'=32,'shard'=8] {'grp'}, dimensions={0} | all-to-all | bytes 17694720 | tf_op jit(solution)/shard_map/all_to_all | solution.py:31
  647.5 27.7 %reshape.17 = bf16[2560,1,1728]{2,1,0:T(2,128)(2,1)} reshape(bf16[32,2,69120]{2,1,0:T(2,128)(2,1)} %all_to_all.8) | data formatting | bytes 17694720
  675.3 14.1 %copy.10 = bf16[1,2560,1728]{2,1,0:T(8,128)(2,1)} copy(bf16[1,2560,1728]{2,0,1:T(2,128)(2,1)} %bitcast.19) | data formatting | bytes 17694720 | tf_op jit(solution)/shard_map/all_to_all | solution.py:31
  689.4 0.0 copy-start
  689.4 0.0 copy-start.1
  689.4 9.7 %convert_reduce_fusion = (f32[80,1728]{1,0:T(8,128)S(1)}, f32[80,1728]{1,0:T(8,128)S(1)}) fusion(bf16[32,80,1728]{2,1,0:T(8,128)(2,1)} %bitcast.20, bf16[32,80,1728]{2,1,0:T(8,128)(2,1)} %param.9), kind=kLoop, calls=%fused_computation.1 | loop fusion | flops 21841920 | bytes 18800640 | tf_op jit(solution)/shard_map/reduce_sum | solution.py:33
  699.1 0.0 copy-done
  699.1 0.0 copy-done.1
  699.1 1.4 divide_subtract_fusion
Async XLA Ops:
  17.8 248.8 %copy-start.2 = (bf16[512,1728]{0,1:T(8,128)(2,1)S(1)}, bf16[512,1728]{0,1:T(8,128)(2,1)}, u32[]{:S(2)}) copy-start(bf16[512,1728]{0,1:T(8,128)(2,1)} %param.6) | copy-start | bytes 5308420
  17.8 248.8 %all-to-all-start = ((bf16[32,80,1728]{2,1,0:T(8,128)(2,1)}), bf16[32,80,1728]{2,1,0:T(8,128)(2,1)}, u32[]{:S(2)}, u32[]{:S(2)}) async-start(bf16[32,80,1728]{2,1,0:T(8,128)(2,1)} %fusion.1), calls=%async_computation | async-start | bytes 18350080 | tf_op jit(solution)/shard_map/all_to_all | solution.py:26
  28.0 108.9 %all-gather.2.cloned.1.call-start = ((), (), s32[]{:S(2)}) async-start(), calls=%async_computation.2 | async-start | bytes 2949120 | tf_op jit(solution)/shard_map/all_gather | solution.py:23
  689.4 9.7 %copy-start = (f32[80,1728]{1,0:T(8,128)S(1)}, f32[80,1728]{1,0:T(8,128)}, u32[]{:S(2)}) copy-start(f32[80,1728]{1,0:T(8,128)} %param.7) | copy-start | bytes 1658884
  689.4 9.8 %copy-start.1 = (f32[80,1728]{1,0:T(8,128)S(1)}, f32[80,1728]{1,0:T(8,128)}, u32[]{:S(2)}) copy-start(f32[80,1728]{1,0:T(8,128)} %param.8) | copy-start | bytes 1658884
Sparse Core Ops, SparseCore 0:
  31.4 105.4 all-gather.1
where the time goes:
time: 710 us; the launch traced here: 707 us
  waiting for transfers between devices  238 us (34%)
  blocking collectives  201 us (28%)
  other arithmetic  123 us (17%)
  local copies, waits for them, and re-layouts  104 us (15%)
  matrix products  17 us (2%)
  between operations  14.1 us (2%)
  starting transfers between devices  10.4 us (1%)
    all_to_all x1, blocking collectives, local(): lax.all_to_all(gradient[None], 'grp', split_axis=1, concat_axis=0, tiled=...  201 us
    all_to_all x1, waiting for transfers between devices, local(): lax.all_to_all(samples, 'grp', split_axis=0, concat_axis=1, tiled=True)[0]  130 us
    all_gather x1, waiting for transfers between devices, local(): group_x = lax.all_gather(tokens, 'shard', axis=0, tiled=True)  108 us
    unnamed x1, other arithmetic  102 us
    unnamed x9, local copies, waits for them, and re-layouts  52.4 us
    broadcast_in_dim x1, local copies, waits for them, and re-layouts, local(): gradient[None]  37.2 us
    dot_general x1, matrix products, contract_rows(): lax.dot_general(left, right, (((0,), (0,)), ((), ())), preferred_element_...  17 us
  transfers between devices with their start and end apart: 2, of which 2 were waited for; matrix products, arithmetic and copies ran while one was open for 0% of the time, Pallas kernels for 0%

commit v1 on v0

--- a/solution.py
+++ b/solution.py
@@ -21,14 +21,17 @@
     noise_vals = weight_noise.astype(jnp.float32)
     samples = (post_mean[None] + post_std[None] * noise_vals).astype(jnp.bfloat16)
     group_x = lax.all_gather(tokens, "shard", axis=0, tiled=True)
+    my_sample = lax.all_to_all(samples, "grp", split_axis=0, concat_axis=0, tiled=True)
     output = jnp.dot(
         group_x,
-        lax.all_to_all(samples, "grp", split_axis=0, concat_axis=1, tiled=True)[0],
+        my_sample.reshape(-1, my_sample.shape[-1]),
         preferred_element_type=jnp.float32,
     )
     residual = (output - target.astype(jnp.float32)).astype(jnp.bfloat16)
     gradient = contract_rows(group_x, residual).astype(jnp.bfloat16)
-    group_grads = lax.all_to_all(gradient[None], "grp", split_axis=1, concat_axis=0, tiled=True)
+    group_grads = lax.all_to_all(
+        gradient.reshape(samples.shape), "grp", split_axis=0, concat_axis=0, tiled=True
+    )
     group_grads = group_grads.astype(jnp.float32)
     mean_grad = jnp.sum(group_grads, axis=0) / groups
     hess_est = jnp.sum(group_grads * noise_vals, axis=0) / groups / post_std

time: 710 us -> 522 us (0.74)
  other arithmetic: 123 us -> 21.8 us
  local copies, waits for them, and re-layouts: 104 us -> 12.7 us
    unnamed x1 -> x0, other arithmetic: 102 us -> none
    unnamed x9 -> x6, local copies, waits for them, and re-layouts: 52.4 us -> 0.01 us
    broadcast_in_dim x1 -> x0, local copies, waits for them, and re-layouts: 37.2 us -> none  [local(): gradient[None]]
    all_to_all x1 -> x0, local copies, waits for them, and re-layouts: 14.1 us -> none  [local(): lax.all_to_all(gradient[None], 'grp', split_axis=1, concat_axis=0, tiled=...]
    convert_element_type x0 -> x1, local copies, waits for them, and re-layouts: none -> 12.7 us  [local(): gradient = contract_rows(group_x, residual).astype(jnp.bfloat16)]
where the time goes in v1:
time: 522 us; the launch traced here: 521 us
  waiting for transfers between devices  239 us (46%)
  blocking collectives  207 us (40%)
  other arithmetic  21.8 us (4%)
  matrix products  17 us (3%)
  between operations  14.1 us (3%)
  local copies, waits for them, and re-layouts  12.7 us (2%)
  starting transfers between devices  10.2 us (2%)
    all_to_all x1, blocking collectives, local(): lax.all_to_all(gradient.reshape(samples.shape), 'grp', split_axis=0, conc...  207 us
    all_to_all x1, waiting for transfers between devices, local(): lax.all_to_all(samples, 'grp', split_axis=0, concat_axis=0, tiled=True)  130 us
    all_gather x1, waiting for transfers between devices, local(): group_x = lax.all_gather(tokens, 'shard', axis=0, tiled=True)  108 us
    dot_general x1, matrix products, contract_rows(): lax.dot_general(left, right, (((0,), (0,)), ((), ())), preferred_element_...  17 us
    convert_element_type x1, local copies, waits for them, and re-layouts, local(): gradient = contract_rows(group_x, residual).astype(jnp.bfloat16)  12.7 us
  transfers between devices with their start and end apart: 2, of which 2 were waited for; matrix products, arithmetic and copies ran while one was open for 0% of the time, Pallas kernels for 0%

profile of v1, /device:TPU:1, one launch (start us, length us, event | category | flops | bytes accessed | tf_op | source)
XLA Modules:
  0.0 521.3 jit_solution(8367304007849500586)
XLA Ops:
  7.2 1.1 multiply_rsqrt_fusion
  8.3 9.5 %fusion.1 = bf16[32,80,1728]{2,1,0:T(8,128)(2,1)} fusion(bf16[32,80,1728]{2,1,0:T(8,128)(2,1)} %param.9, f32[80,1728]{1,0:T(8,128)S(1)} %multiply_rsqrt_fusion, f32[80,1728]{1,0:T(8,128)} %param.7), kind=kLoop, calls=%fused_computation.4 | loop fusion | flops 17694720 | bytes 18800640 | tf_op jit(solution)/shard_map/convert_element_type | solution.py:22
  17.8 0.0 copy-start.2
  17.8 10.2 %all-to-all-start = ((bf16[32,80,1728]{2,1,0:T(8,128)(2,1)}), bf16[32,80,1728]{2,1,0:T(8,128)(2,1)}, u32[]{:S(2)}, u32[]{:S(2)}) async-start(bf16[32,80,1728]{2,1,0:T(8,128)(2,1)} %fusion.1), calls=%async_computation | async-start | bytes 18350080 | tf_op jit(solution)/shard_map/all_to_all | solution.py:24
  28.0 0.0 all-gather.2.cloned.1.call-start
  28.0 0.7 all-gather.2.cloned.1.call-update
  28.7 108.1 %all-gather.2.cloned.1.call-done = bf16[512,2560]{1,0:T(8,128)(2,1)} async-done(((bf16[64,2560]{1,0:T(8,128)(2,1)}), bf16[512,2560]{1,0:T(8,128)(2,1)}) %all-gather.2.cloned.1.call-update) | async-done | bytes 2621456 | tf_op jit(solution)/shard_map/all_gather | solution.py:23
  136.9 129.7 %all-to-all-done = bf16[32,80,1728]{2,1,0:T(8,128)(2,1)} async-done(((bf16[32,80,1728]{2,1,0:T(8,128)(2,1)}), bf16[32,80,1728]{2,1,0:T(8,128)(2,1)}, u32[]{:S(2)}, u32[]{:S(2)}) %all-to-all-start) | async-done | bytes 8847392 | tf_op jit(solution)/shard_map/all_to_all | solution.py:24
  266.6 0.0 copy-done.2
  266.6 17.0 %fusion.3 = bf16[2560,1728]{0,1:T(8,128)(2,1)} fusion(bf16[512,2560]{1,0:T(8,128)(2,1)} %all-gather.2.cloned.1.call-done, bf16[512,1728]{0,1:T(8,128)(2,1)S(1)} %copy-done.2, bf16[2560,1728]{1,0:T(8,128)(2,1)} %bitcast), kind=kOutput, calls=%fused_computation.7 | convolution fusion | flops 9066774528 | bytes 22085632 | tf_op jit(solution)/shard_map/dot_general | solution.py:13
  283.6 12.7 %copy.8 = bf16[2560,1728]{1,0:T(8,128)(2,1)} copy(bf16[2560,1728]{0,1:T(8,128)(2,1)} %fusion.3) | data formatting | bytes 17694720 | tf_op jit(solution)/shard_map/convert_element_type | solution.py:31
  296.2 207.0 %all_to_all.10 = bf16[32,80,1728]{2,1,0:T(8,128)(2,1)} all-to-all(bf16[32,80,1728]{2,1,0:T(8,128)(2,1)} %bitcast.13), channel_id=1, replica_groups=mesh['grp'=32,'shard'=8] {'grp'}, dimensions={0} | all-to-all | bytes 17694720 | tf_op jit(solution)/shard_map/all_to_all | solution.py:32
  503.3 0.0 copy-start
  503.3 0.0 copy-start.1
  503.3 9.7 %convert_reduce_fusion = (f32[80,1728]{1,0:T(8,128)S(1)}, f32[80,1728]{1,0:T(8,128)S(1)}) fusion(bf16[32,80,1728]{2,1,0:T(8,128)(2,1)} %all_to_all.10, bf16[32,80,1728]{2,1,0:T(8,128)(2,1)} %param.9), kind=kLoop, calls=%fused_computation.1 | loop fusion | flops 21841920 | bytes 18800640 | tf_op jit(solution)/shard_map/reduce_sum | solution.py:36
  513.0 0.0 copy-done
  513.0 0.0 copy-done.1
  513.0 1.4 divide_subtract_fusion
Async XLA Ops:
  17.8 248.8 %copy-start.2 = (bf16[512,1728]{0,1:T(8,128)(2,1)S(1)}, bf16[512,1728]{0,1:T(8,128)(2,1)}, u32[]{:S(2)}) copy-start(bf16[512,1728]{0,1:T(8,128)(2,1)} %param.6) | copy-start | bytes 5308420
  17.8 248.8 %all-to-all-start = ((bf16[32,80,1728]{2,1,0:T(8,128)(2,1)}), bf16[32,80,1728]{2,1,0:T(8,128)(2,1)}, u32[]{:S(2)}, u32[]{:S(2)}) async-start(bf16[32,80,1728]{2,1,0:T(8,128)(2,1)} %fusion.1), calls=%async_computation | async-start | bytes 18350080 | tf_op jit(solution)/shard_map/all_to_all | solution.py:24
  28.0 108.9 %all-gather.2.cloned.1.call-start = ((), (), s32[]{:S(2)}) async-start(), calls=%async_computation.2 | async-start | bytes 2949120 | tf_op jit(solution)/shard_map/all_gather | solution.py:23
  503.3 9.7 %copy-start = (f32[80,1728]{1,0:T(8,128)S(1)}, f32[80,1728]{1,0:T(8,128)}, u32[]{:S(2)}) copy-start(f32[80,1728]{1,0:T(8,128)} %param.7) | copy-start | bytes 1658884
  503.3 9.8 %copy-start.1 = (f32[80,1728]{1,0:T(8,128)S(1)}, f32[80,1728]{1,0:T(8,128)}, u32[]{:S(2)}) copy-start(f32[80,1728]{1,0:T(8,128)} %param.8) | copy-start | bytes 1658884
Sparse Core Ops, SparseCore 0:
  31.4 105.4 all-gather.1

commit v2 on v0

--- a/solution.py
+++ b/solution.py
@@ -15,21 +15,39 @@
     )
 
 
+def column_chunks(width):
+    first = min(width, ((width // 2 + 127) // 128) * 128)
+    return [(0, first), (first, width)] if first < width else [(0, width)]
+
+
 def local(tokens, target, post_mean, post_hess, weight_noise):
     groups = weight_noise.shape[0]
     post_std = lax.rsqrt(sample_size * (post_hess + weight_decay))
+    group_x = lax.all_gather(tokens, "shard", axis=0, tiled=True)
+    chunks = column_chunks(weight_noise.shape[-1])
+    my_samples = []
+    for lo, hi in chunks:
+        noise_vals = weight_noise[:, :, lo:hi].astype(jnp.float32)
+        samples = (post_mean[None, :, lo:hi] + post_std[None, :, lo:hi] * noise_vals).astype(
+            jnp.bfloat16
+        )
+        my_samples.append(lax.all_to_all(samples, "grp", split_axis=0, concat_axis=0, tiled=True))
+    grads = []
+    for (lo, hi), my_sample in zip(chunks, my_samples):
+        output = jnp.dot(
+            group_x,
+            my_sample.reshape(-1, hi - lo),
+            preferred_element_type=jnp.float32,
+        )
+        residual = (output - target[:, lo:hi].astype(jnp.float32)).astype(jnp.bfloat16)
+        gradient = contract_rows(group_x, residual).astype(jnp.bfloat16)
+        grads.append(
+            lax.all_to_all(
+                gradient.reshape(my_sample.shape), "grp", split_axis=0, concat_axis=0, tiled=True
+            )
+        )
+    group_grads = jnp.concatenate(grads, axis=-1).astype(jnp.float32)
     noise_vals = weight_noise.astype(jnp.float32)
-    samples = (post_mean[None] + post_std[None] * noise_vals).astype(jnp.bfloat16)
-    group_x = lax.all_gather(tokens, "shard", axis=0, tiled=True)
-    output = jnp.dot(
-        group_x,
-        lax.all_to_all(samples, "grp", split_axis=0, concat_axis=1, tiled=True)[0],
-        preferred_element_type=jnp.float32,
-    )
-    residual = (output - target.astype(jnp.float32)).astype(jnp.bfloat16)
-    gradient = contract_rows(group_x, residual).astype(jnp.bfloat16)
-    group_grads = lax.all_to_all(gradient[None], "grp", split_axis=1, concat_axis=0, tiled=True)
-    group_grads = group_grads.astype(jnp.float32)
     mean_grad = jnp.sum(group_grads, axis=0) / groups
     hess_est = jnp.sum(group_grads * noise_vals, axis=0) / groups / post_std
     keep_rate = 1.0 - hess_decay

time: 710 us -> 505 us (0.71)
  other arithmetic: 123 us -> 21.4 us
  blocking collectives: 201 us -> 110 us
  local copies, waits for them, and re-layouts: 104 us -> 15.4 us
  waiting for transfers between devices: 238 us -> 299 us
  starting transfers between devices: 10.4 us -> 23.5 us
    unnamed x1 -> x0, other arithmetic: 102 us -> none
    all_to_all x1, blocking collectives: 201 us -> 110 us  [local(): lax.all_to_all(gradient.reshape(my_sample.shape), 'grp', split_axis=0, co...]
    all_to_all x1 -> x3, waiting for transfers between devices: 130 us -> 188 us  [the longest x2 103 us: local(): lax.all_to_all(samples, 'grp', split_axis=0, concat_axis=0, tiled=True)]
    unnamed x9 -> x6, local copies, waits for them, and re-layouts: 52.4 us -> 0.01 us
    broadcast_in_dim x1 -> x0, local copies, waits for them, and re-layouts: 37.2 us -> none  [local(): gradient[None]]
    convert_element_type x0 -> x2, local copies, waits for them, and re-layouts: none -> 14.4 us  [local(): gradient = contract_rows(group_x, residual).astype(jnp.bfloat16)]
    all_to_all x1 -> x0, local copies, waits for them, and re-layouts: 14.1 us -> none  [local(): lax.all_to_all(gradient[None], 'grp', split_axis=1, concat_axis=0, tiled=...]
    all_to_all x1 -> x3, starting transfers between devices: 10.2 us -> 23.4 us  [the longest x2 16.8 us: local(): lax.all_to_all(samples, 'grp', split_axis=0, concat_axis=0, tiled=True)]
  transfers between devices with their start and end apart: 2 -> 4, of which waited for: 2 -> 4; matrix products, arithmetic and copies ran while one was open for 0% -> 8% of each run, Pallas kernels for 0% -> 0%
where the time goes in v2:
time: 505 us; the launch traced here: 504 us
  waiting for transfers between devices  299 us (59%)
  blocking collectives  110 us (22%)
  starting transfers between devices  23.5 us (5%)
  other arithmetic  21.4 us (4%)
  matrix products  20.7 us (4%)
  local copies, waits for them, and re-layouts  15.4 us (3%)
  between operations  14.1 us (3%)
    all_gather x1, waiting for transfers between devices, local(): group_x = lax.all_gather(tokens, 'shard', axis=0, tiled=True)  110 us
    all_to_all x1, blocking collectives, local(): lax.all_to_all(gradient.reshape(my_sample.shape), 'grp', split_axis=0, co...  110 us
    all_to_all x2, waiting for transfers between devices, local(): lax.all_to_all(samples, 'grp', split_axis=0, concat_axis=0, tiled=True)  103 us
    all_to_all x1, waiting for transfers between devices, local(): lax.all_to_all(gradient.reshape(my_sample.shape), 'grp', split_axis=0, co...  84.8 us
    dot_general x2, matrix products, contract_rows(): lax.dot_general(left, right, (((0,), (0,)), ((), ())), preferred_element_...  20.7 us
    all_to_all x2, starting transfers between devices, local(): lax.all_to_all(samples, 'grp', split_axis=0, concat_axis=0, tiled=True)  16.8 us
    convert_element_type x2, local copies, waits for them, and re-layouts, local(): gradient = contract_rows(group_x, residual).astype(jnp.bfloat16)  14.4 us
    convert_element_type x2, other arithmetic, local(): (post_mean[None, :, lo:hi] + post_std[None, :, lo:hi] * noise_vals).astyp...  11.2 us
  transfers between devices with their start and end apart: 4, of which 4 were waited for; matrix products, arithmetic and copies ran while one was open for 8% of the time, Pallas kernels for 0%

profile of v2, /device:TPU:1, one launch (start us, length us, event | category | flops | bytes accessed | tf_op | source)
XLA Modules:
  0.0 504.5 jit_solution(201361145258455535)
XLA Ops:
  7.2 1.0 slice.28
  8.1 1.1 multiply_rsqrt_fusion
  9.3 5.5 %add_convert_fusion = bf16[32,80,832]{2,1,0:T(8,128)(2,1)} fusion(bf16[32,80,1728]{2,1,0:T(8,128)(2,1)} %param.9, f32[80,832]{1,0:T(8,128)S(1)} %slice.33, f32[80,832]{1,0:T(8,128)S(1)} %slice.28), kind=kLoop, calls=%fused_computation.4 | loop fusion | flops 8519680 | bytes 9052160 | tf_op jit(solution)/shard_map/convert_element_type | solution.py:31
  14.9 0.0 slice-start
  14.9 10.2 %all-to-all-start.2 = ((bf16[32,80,832]{2,1,0:T(8,128)(2,1)}), bf16[32,80,832]{2,1,0:T(8,128)(2,1)}, u32[]{:S(2)}, u32[]{:S(2)}) async-start(bf16[32,80,832]{2,1,0:T(8,128)(2,1)} %add_convert_fusion), calls=%async_computation.2 | async-start | bytes 9175040 | tf_op jit(solution)/shard_map/all_to_all | solution.py:34
  25.1 0.0 slice-done
  25.1 5.7 %add_convert_fusion.1 = bf16[32,80,896]{2,1,0:T(8,128)(2,1)} fusion(bf16[32,80,1728]{2,1,0:T(8,128)(2,1)} %param.9, f32[80,896]{1,0:T(8,128)S(1)} %slice.32, f32[80,896]{1,0:T(8,128)S(1)} %slice-done), kind=kLoop, calls=%fused_computation.5 | loop fusion | flops 9175040 | bytes 9748480 | tf_op jit(solution)/shard_map/convert_element_type | solution.py:31
  30.8 95.9 %all-to-all-done.2 = bf16[32,80,832]{2,1,0:T(8,128)(2,1)} async-done(((bf16[32,80,832]{2,1,0:T(8,128)(2,1)}), bf16[32,80,832]{2,1,0:T(8,128)(2,1)}, u32[]{:S(2)}, u32[]{:S(2)}) %all-to-all-start.2) | async-done | bytes 4259872 | tf_op jit(solution)/shard_map/all_to_all | solution.py:34
  126.7 6.6 %all-to-all-start = ((bf16[32,80,896]{2,1,0:T(8,128)(2,1)}), bf16[32,80,896]{2,1,0:T(8,128)(2,1)}, u32[]{:S(2)}, u32[]{:S(2)}) async-start(bf16[32,80,896]{2,1,0:T(8,128)(2,1)} %add_convert_fusion.1), calls=%async_computation | async-start | bytes 9175040 | tf_op jit(solution)/shard_map/all_to_all | solution.py:34
  133.3 0.0 all-gather.2.cloned.1.call-start
  133.4 0.7 all-gather.2.cloned.1.call-update
  134.1 110.5 %all-gather.2.cloned.1.call-done = bf16[512,2560]{1,0:T(8,128)(2,1)} async-done(((bf16[64,2560]{1,0:T(8,128)(2,1)}), bf16[512,2560]{1,0:T(8,128)(2,1)}) %all-gather.2.cloned.1.call-update) | async-done | bytes 2621456 | tf_op jit(solution)/shard_map/all_gather | solution.py:26
  244.5 11.1 %fusion.2 = bf16[2560,832]{0,1:T(8,128)(2,1)} fusion(bf16[512,2560]{1,0:T(8,128)(2,1)} %all-gather.2.cloned.1.call-done, bf16[2560,832]{1,0:T(8,128)(2,1)} %bitcast.4, bf16[512,1728]{0,1:T(8,128)(2,1)} %param.6), kind=kOutput, calls=%fused_computation.9 | convolution fusion | flops 4365484032 | bytes 14942208 | tf_op jit(solution)/shard_map/dot_general | solution.py:13
  255.6 7.1 %copy.10 = bf16[2560,832]{1,0:T(8,128)(2,1)} copy(bf16[2560,832]{0,1:T(8,128)(2,1)} %fusion.2) | data formatting | bytes 8519680 | tf_op jit(solution)/shard_map/convert_element_type | solution.py:43
  262.8 7.3 %all-to-all-done = bf16[32,80,896]{2,1,0:T(8,128)(2,1)} async-done(((bf16[32,80,896]{2,1,0:T(8,128)(2,1)}), bf16[32,80,896]{2,1,0:T(8,128)(2,1)}, u32[]{:S(2)}, u32[]{:S(2)}) %all-to-all-start) | async-done | bytes 4587552 | tf_op jit(solution)/shard_map/all_to_all | solution.py:34
  270.1 0.0 copy-start.2
  270.1 6.6 %all-to-all-start.3 = ((bf16[32,80,832]{2,1,0:T(8,128)(2,1)}), bf16[32,80,832]{2,1,0:T(8,128)(2,1)}, u32[]{:S(2)}, u32[]{:S(2)}) async-start(bf16[32,80,832]{2,1,0:T(8,128)(2,1)} %bitcast.26), calls=%async_computation.3 | async-start | bytes 9175040 | tf_op jit(solution)/shard_map/all_to_all | solution.py:45
  276.8 0.0 copy-done.2
  276.8 9.6 %fusion.1 = bf16[2560,896]{0,1:T(8,128)(2,1)} fusion(bf16[512,2560]{1,0:T(8,128)(2,1)S(1)} %copy-done.2, bf16[2560,896]{1,0:T(8,128)(2,1)} %bitcast, bf16[512,1728]{0,1:T(8,128)(2,1)} %param.6), kind=kOutput, calls=%fused_computation.8 | convolution fusion | flops 4701290496 | bytes 15335424 | tf_op jit(solution)/shard_map/dot_general | solution.py:13
  286.4 7.2 %copy.9 = bf16[2560,896]{1,0:T(8,128)(2,1)} copy(bf16[2560,896]{0,1:T(8,128)(2,1)} %fusion.1) | data formatting | bytes 9175040 | tf_op jit(solution)/shard_map/convert_element_type | solution.py:43
  293.6 84.8 %all-to-all-done.3 = bf16[32,80,832]{2,1,0:T(8,128)(2,1)} async-done(((bf16[32,80,832]{2,1,0:T(8,128)(2,1)}), bf16[32,80,832]{2,1,0:T(8,128)(2,1)}, u32[]{:S(2)}, u32[]{:S(2)}) %all-to-all-start.3) | async-done | bytes 4259872 | tf_op jit(solution)/shard_map/all_to_all | solution.py:45
  378.4 110.2 %all_to_all.20 = bf16[32,80,896]{2,1,0:T(8,128)(2,1)S(1)} all-to-all(bf16[32,80,896]{2,1,0:T(8,128)(2,1)} %bitcast.27), channel_id=1, replica_groups=mesh['grp'=32,'shard'=8] {'grp'}, dimensions={0} | all-to-all | bytes 9175040 | tf_op jit(solution)/shard_map/all_to_all | solution.py:45
  488.6 0.0 copy-start
  488.6 0.0 copy-start.1
  488.6 7.6 %convert_reduce_fusion = (f32[80,1728]{1,0:T(8,128)S(1)}, f32[80,1728]{1,0:T(8,128)S(1)}) fusion(bf16[32,80,832]{2,1,0:T(8,128)(2,1)} %all-to-all-done.3, bf16[32,80,896]{2,1,0:T(8,128)(2,1)S(1)} %all_to_all.20, bf16[32,80,1728]{2,1,0:T(8,128)(2,1)} %param.9), kind=kLoop, calls=%fused_computation.1 | loop fusion | flops 35112960 | bytes 18800640 | tf_op jit(solution)/shard_map/reduce_sum | solution.py:51
  496.2 0.0 copy-done
  496.2 0.0 copy-done.1
  496.2 1.4 divide_subtract_fusion
  (2 shorter events, 0.0 us)
Async XLA Ops:
  14.9 10.2 %slice-start = ((f32[80,1728]{1,0:T(8,128)}), f32[80,896]{1,0:T(8,128)S(1)}, s32[]{:S(2)}) async-start(f32[80,1728]{1,0:T(8,128)} %param.7), calls=%async_computation.5 | async-start | bytes 573440 | tf_op jit(solution)/shard_map/slice | solution.py:31
  14.9 111.8 %all-to-all-start.2 = ((bf16[32,80,832]{2,1,0:T(8,128)(2,1)}), bf16[32,80,832]{2,1,0:T(8,128)(2,1)}, u32[]{:S(2)}, u32[]{:S(2)}) async-start(bf16[32,80,832]{2,1,0:T(8,128)(2,1)} %add_convert_fusion), calls=%async_computation.2 | async-start | bytes 9175040 | tf_op jit(solution)/shard_map/all_to_all | solution.py:34
  126.7 143.4 %all-to-all-start = ((bf16[32,80,896]{2,1,0:T(8,128)(2,1)}), bf16[32,80,896]{2,1,0:T(8,128)(2,1)}, u32[]{:S(2)}, u32[]{:S(2)}) async-start(bf16[32,80,896]{2,1,0:T(8,128)(2,1)} %add_convert_fusion.1), calls=%async_computation | async-start | bytes 9175040 | tf_op jit(solution)/shard_map/all_to_all | solution.py:34
  133.3 111.2 %all-gather.2.cloned.1.call-start = ((), (), s32[]{:S(2)}) async-start(), calls=%async_computation.4 | async-start | bytes 2949120 | tf_op jit(solution)/shard_map/all_gather | solution.py:26
  270.1 6.7 %copy-start.2 = (bf16[512,2560]{1,0:T(8,128)(2,1)S(1)}, bf16[512,2560]{1,0:T(8,128)(2,1)}, u32[]{:S(2)}) copy-start(bf16[512,2560]{1,0:T(8,128)(2,1)} %all-gather.2.cloned.1.call-done) | copy-start | bytes 7864324
  270.1 108.3 %all-to-all-start.3 = ((bf16[32,80,832]{2,1,0:T(8,128)(2,1)}), bf16[32,80,832]{2,1,0:T(8,128)(2,1)}, u32[]{:S(2)}, u32[]{:S(2)}) async-start(bf16[32,80,832]{2,1,0:T(8,128)(2,1)} %bitcast.26), calls=%async_computation.3 | async-start | bytes 9175040 | tf_op jit(solution)/shard_map/all_to_all | solution.py:45
  488.6 7.6 %copy-start = (f32[80,1728]{1,0:T(8,128)S(1)}, f32[80,1728]{1,0:T(8,128)}, u32[]{:S(2)}) copy-start(f32[80,1728]{1,0:T(8,128)} %param.7) | copy-start | bytes 1658884
  488.6 7.6 %copy-start.1 = (f32[80,1728]{1,0:T(8,128)S(1)}, f32[80,1728]{1,0:T(8,128)}, u32[]{:S(2)}) copy-start(f32[80,1728]{1,0:T(8,128)} %param.8) | copy-start | bytes 1658884
Sparse Core Ops, SparseCore 0:
  136.7 107.7 all-gather.1

commit v3 on v2

v3 whole, which is shorter than its diff:
```python
import jax
import jax.numpy as jnp
from jax import lax
from jax.sharding import Mesh, PartitionSpec as P

sample_size = 50.0
weight_decay = 0.02
hess_decay = 0.95
learn_rate = 0.3
Z_LINE = 4


def contract_rows(left, right):
    return lax.dot_general(
        left, right, (((0,), (0,)), ((), ())), preferred_element_type=jnp.float32
    )


def column_chunks(width):
    first = min(width, ((width // 2 + 127) // 128) * 128)
    return [(0, first), (first, width)] if first < width else [(0, width)]


def local(tokens, target, post_mean, post_hess, weight_noise):
    groups, rows, width = weight_noise.shape
    nz = Z_LINE
    nxc = groups // nz
    me = lax.axis_index("zl")
    post_std = lax.rsqrt(sample_size * (post_hess + weight_decay))
    group_x = lax.all_gather(tokens, "shard", axis=0, tiled=True)
    doubled = jnp.concatenate([group_x, group_x], axis=1)
    plane = group_x.shape[1] // nz
    x_r = lax.dynamic_slice_in_dim(doubled, me * plane, group_x.shape[1], axis=1)
    chunks = column_chunks(width)
    staged = []
    for lo, hi in chunks:
        noise_vals = weight_noise[:, :, lo:hi].astype(jnp.float32)
        samples = (post_mean[None, :, lo:hi] + post_std[None, :, lo:hi] * noise_vals).astype(
            jnp.bfloat16
        )
        s4 = samples.reshape(nz, nxc, rows, hi - lo)
        staged.append(lax.all_to_all(s4, "xc", split_axis=1, concat_axis=1, tiled=True))
    grads = []
    for (lo, hi), t1 in zip(chunks, staged):
        blocks = [t1[me]]
        for e in range(1, nz):
            part = lax.dynamic_index_in_dim(t1, (me - e) % nz, axis=0, keepdims=False)
            perm = [(src, (src - e) % nz) for src in range(nz)]
            blocks.append(lax.ppermute(part, "zl", perm))
        full = jnp.stack(blocks).reshape(-1, hi - lo)
        output = jnp.dot(x_r, full, preferred_element_type=jnp.float32)
        residual = (output - target[:, lo:hi].astype(jnp.float32)).astype(jnp.bfloat16)
        grad_r = contract_rows(x_r, residual).astype(jnp.bfloat16).reshape(nz, nxc, rows, hi - lo)
        back = [grad_r[0]]
        for e in range(1, nz):
            perm = [(src, (src + e) % nz) for src in range(nz)]
            back.append(lax.ppermute(grad_r[e], "zl", perm))
        q = jnp.stack(back)
        grads.append(lax.all_to_all(q, "xc", split_axis=1, concat_axis=1, tiled=True))
    group_grads = jnp.concatenate(grads, axis=-1).astype(jnp.float32)
    order = (me - jnp.arange(nz)) % nz
    noise_r = jnp.take(weight_noise.reshape(nz, nxc, rows, width), order, axis=0)
    mean_grad = jnp.sum(group_grads, axis=(0, 1)) / groups
    hess_est = (
        jnp.sum(group_grads * noise_r.astype(jnp.float32), axis=(0, 1)) / groups / post_std
    )
    keep_rate = 1.0 - hess_decay
    gap = post_hess - hess_est
    new_hess = (
        hess_decay * post_hess
        + keep_rate * hess_est
        + 0.5 * keep_rate * keep_rate * gap * gap / (post_hess + weight_decay)
    )
    new_mean = post_mean - learn_rate * (mean_grad + weight_decay * post_mean) / (
        new_hess + weight_decay
    )
    return (new_mean, new_hess)


def solution(mesh):
    n_grp = mesh.shape["grp"]
    fine = Mesh(
        mesh.devices.reshape(Z_LINE, n_grp // Z_LINE, mesh.shape["shard"]),
        ("zl", "xc", "shard"),
    )
    grp = ("zl", "xc")
    return jax.shard_map(
        local,
        mesh=fine,
        in_specs=(
            P(("zl", "xc", "shard"), None),
            P(grp, "shard"),
            P(grp, "shard"),
            P(grp, "shard"),
            P(None, grp, "shard"),
        ),
        out_specs=(P(grp, "shard"), P(grp, "shard")),
        check_vma=False,
    )
```

time: 505 us -> 616 us (1.22)
  waiting for transfers between devices: 299 us -> 410 us
  blocking collectives: 110 us -> 0 us
  starting transfers between devices: 23.5 us -> 85.5 us
  local copies, waits for them, and re-layouts: 15.4 us -> 53.9 us
  other arithmetic: 21.4 us -> 29.6 us
    ppermute x0 -> x12, waiting for transfers between devices: none -> 324 us  [the longest x6 165 us: local(): blocks.append(lax.ppermute(part, 'zl', perm))]
    all_gather x1, waiting for transfers between devices: 110 us -> 0.01 us  [local(): group_x = lax.all_gather(tokens, 'shard', axis=0, tiled=True)]
    all_to_all x1 -> x0, blocking collectives: 110 us -> none  [local(): lax.all_to_all(gradient.reshape(my_sample.shape), 'grp', split_axis=0, co...]
    all_to_all x3 -> x4, waiting for transfers between devices: 188 us -> 84.5 us  [the longest x2 52.2 us: local(): lax.all_to_all(s4, 'xc', split_axis=1, concat_axis=1, tiled=True)]
    ppermute x0 -> x12, starting transfers between devices: none -> 60.3 us  [the longest x6 53.8 us: local(): back.append(lax.ppermute(grad_r[e], 'zl', perm))]
    gather x0 -> x4, local copies, waits for them, and re-layouts: none -> 20.6 us  [local(): jnp.take(weight_noise.reshape(nz, nxc, rows, width), order, axis=0)]
    convert_element_type x2 -> x0, local copies, waits for them, and re-layouts: 14.4 us -> none  [local(): gradient = contract_rows(group_x, residual).astype(jnp.bfloat16)]
    slice x0 -> x8, local copies, waits for them, and re-layouts: none -> 13.1 us  [the longest x3 7.29 us: local(): back = [grad_r[0]]]
  transfers between devices with their start and end apart: 4 -> 17, of which waited for: 4 -> 10; matrix products, arithmetic and copies ran while one was open for 8% -> 14% of each run, Pallas kernels for 0% -> 0%
where the time goes in v3:
time: 616 us; the launch traced here: 615 us
  waiting for transfers between devices  410 us (67%)
  starting transfers between devices  85.5 us (14%)
  local copies, waits for them, and re-layouts  53.9 us (9%)
  other arithmetic  29.6 us (5%)
  matrix products  22.1 us (4%)
  between operations  14.2 us (2%)
    ppermute x6, waiting for transfers between devices, local(): blocks.append(lax.ppermute(part, 'zl', perm))  165 us
    ppermute x6, waiting for transfers between devices, local(): back.append(lax.ppermute(grad_r[e], 'zl', perm))  160 us
    ppermute x6, starting transfers between devices, local(): back.append(lax.ppermute(grad_r[e], 'zl', perm))  53.8 us
    all_to_all x2, waiting for transfers between devices, local(): lax.all_to_all(s4, 'xc', split_axis=1, concat_axis=1, tiled=True)  52.2 us
    all_to_all x2, waiting for transfers between devices, local(): lax.all_to_all(q, 'xc', split_axis=1, concat_axis=1, tiled=True)  32.3 us
    dot_general x2, matrix products, contract_rows(): lax.dot_general(left, right, (((0,), (0,)), ((), ())), preferred_element_...  22.1 us
    gather x4, local copies, waits for them, and re-layouts, local(): jnp.take(weight_noise.reshape(nz, nxc, rows, width), order, axis=0)  20.6 us
    all_to_all x2, starting transfers between devices, local(): lax.all_to_all(s4, 'xc', split_axis=1, concat_axis=1, tiled=True)  14 us
  transfers between devices with their start and end apart: 17, of which 10 were waited for; matrix products, arithmetic and copies ran while one was open for 14% of the time, Pallas kernels for 0%

profile of v3, /device:TPU:1, one launch (start us, length us, event | category | flops | bytes accessed | tf_op | source)
XLA Modules:
  0.0 614.8 jit_solution(11588544482893203958)
XLA Ops:
  9.3 3.5 add_convert_fusion
  15.4 7.7 %all-to-all-start.2 = ((bf16[4,8,80,832]{3,2,0,1:T(8,128)(2,1)}), bf16[4,8,80,832]{3,2,0,1:T(8,128)(2,1)}, u32[]{:S(2)}, u32[]{:S(2)}) async-start(bf16[4,8,80,832]{3,2,0,1:T(8,128)(2,1)} %copy.26), calls=%async_computation.2 | async-start | bytes 9175040 | tf_op jit(solution)/shard_map/all_to_all | solution.py:42
  23.8 52.2 %all-to-all-done.2 = bf16[4,8,80,832]{3,2,0,1:T(8,128)(2,1)} async-done(((bf16[4,8,80,832]{3,2,0,1:T(8,128)(2,1)}), bf16[4,8,80,832]{3,2,0,1:T(8,128)(2,1)}, u32[]{:S(2)}, u32[]{:S(2)}) %all-to-all-start.2) | async-done | bytes 4259872 | tf_op jit(solution)/shard_map/all_to_all | solution.py:42
  76.1 4.0 constant_dynamic-slice_fusion
  80.1 2.9 collective-permute-start.7
  83.8 3.4 add_convert_fusion.1
  89.8 6.3 %all-to-all-start = ((bf16[4,8,80,896]{3,2,0,1:T(8,128)(2,1)}), bf16[4,8,80,896]{3,2,0,1:T(8,128)(2,1)}, u32[]{:S(2)}, u32[]{:S(2)}) async-start(bf16[4,8,80,896]{3,2,0,1:T(8,128)(2,1)} %copy.22), calls=%async_computation | async-start | bytes 9175040 | tf_op jit(solution)/shard_map/all_to_all | solution.py:42
  96.1 24.2 %collective-permute-done.8 = bf16[8,80,832]{2,1,0:T(8,128)(2,1)} collective-permute-done((bf16[8,80,832]{2,1,0:T(8,128)(2,1)}, bf16[8,80,832]{2,1,0:T(8,128)(2,1)}, u32[]{:S(2)}, u32[]{:S(2)}) %collective-permute-start.8) | collective-permute-done | bytes 1064992 | tf_op jit(solution)/shard_map/ppermute | solution.py:49
  120.4 53.7 %collective-permute-done.7 = bf16[8,80,832]{2,1,0:T(8,128)(2,1)} collective-permute-done((bf16[8,80,832]{2,1,0:T(8,128)(2,1)}, bf16[8,80,832]{2,1,0:T(8,128)(2,1)}, u32[]{:S(2)}, u32[]{:S(2)}) %collective-permute-start.7) | collective-permute-done | bytes 1064992 | tf_op jit(solution)/shard_map/ppermute | solution.py:49
  179.0 10.5 %convolution_convert_fusion.1 = bf16[2560,832]{0,1:T(8,128)(2,1)} fusion(bf16[2560,832]{1,0:T(8,128)(2,1)} %bitcast.52, bf16[512,1728]{0,1:T(8,128)(2,1)S(1)} %copy-done, s32[]{:T(128)S(6)} %select_n.79, bf16[512,2560]{1,0:T(8,128)(2,1)} %all-gather.2.cloned.1.call-done), kind=kOutput, calls=%fused_computation.12 | convolution fusion | flops 4375969792 | bytes 14943232 | tf_op jit(solution)/shard_map/dot_general | solution.py:14
  189.5 3.6 fusion.13
  195.5 24.8 %collective-permute-start.9 = (bf16[8,80,832]{2,1,0:T(8,128)(2,1)}, bf16[8,80,832]{2,1,0:T(8,128)(2,1)}, u32[]{:S(2)}, u32[]{:S(2)}) collective-permute-start(bf16[8,80,832]{2,1,0:T(8,128)(2,1)} %bitcast.60), channel_id=1, source_target_pairs={{0,64},{64,128},{128,192},{192,0},{1,65},{65,129},{129,193},{193,1... | collective-permute-start | bytes 3194888 | tf_op jit(solution)/shard_map/ppermute | solution.py:57
  225.7 4.2 dynamic-slice_bitcast_fusion.6
  231.7 13.3 %collective-permute-done.9 = bf16[8,80,832]{2,1,0:T(8,128)(2,1)} collective-permute-done((bf16[8,80,832]{2,1,0:T(8,128)(2,1)}, bf16[8,80,832]{2,1,0:T(8,128)(2,1)}, u32[]{:S(2)}, u32[]{:S(2)}) %collective-permute-start.9) | collective-permute-done | bytes 1064992 | tf_op jit(solution)/shard_map/ppermute | solution.py:57
  247.2 48.6 %collective-permute-done.10 = bf16[8,80,832]{2,1,0:T(8,128)(2,1)} collective-permute-done((bf16[8,80,832]{2,1,0:T(8,128)(2,1)}, bf16[8,80,832]{2,1,0:T(8,128)(2,1)}, u32[]{:S(2)}, u32[]{:S(2)}) %collective-permute-start.10) | collective-permute-done | bytes 1064992 | tf_op jit(solution)/shard_map/ppermute | solution.py:57
  298.2 2.6 copy.32
  300.8 5.3 all-to-all-start.3
  306.7 12.2 %collective-permute-done.2 = bf16[8,80,896]{2,1,0:T(8,128)(2,1)} collective-permute-done((bf16[8,80,896]{2,1,0:T(8,128)(2,1)}, bf16[8,80,896]{2,1,0:T(8,128)(2,1)}, u32[]{:S(2)}, u32[]{:S(2)}) %collective-permute-start.2) | collective-permute-done | bytes 1146912 | tf_op jit(solution)/shard_map/ppermute | solution.py:49
  318.8 74.5 %collective-permute-done.1 = bf16[8,80,896]{2,1,0:T(8,128)(2,1)} collective-permute-done((bf16[8,80,896]{2,1,0:T(8,128)(2,1)}, bf16[8,80,896]{2,1,0:T(8,128)(2,1)}, u32[]{:S(2)}, u32[]{:S(2)}) %collective-permute-start.1) | collective-permute-done | bytes 1146912 | tf_op jit(solution)/shard_map/ppermute | solution.py:49
  393.3 3.9 pad_maximum_fusion.1
  397.2 11.6 %convolution_convert_fusion = bf16[2560,896]{1,0:T(8,128)(2,1)} fusion(bf16[512,896]{1,0:T(8,128)(2,1)S(1)} %copy.37, bf16[2560,896]{1,0:T(8,128)(2,1)} %bitcast.51, s32[]{:T(128)S(6)} %select_n.79, bf16[512,2560]{1,0:T(8,128)(2,1)} %all-gather.2.cloned.1.call-done), kind=kOutput, calls=%fused_computation.9 | convolution fusion | flops 4711776256 | bytes 15336448 | tf_op jit(solution)/shard_map/dot_general | solution.py:14
  408.8 2.7 fusion.12
  411.5 26.6 %collective-permute-start.5 = (bf16[8,80,896]{2,1,0:T(8,128)(2,1)S(1)}, bf16[8,80,896]{2,1,0:T(8,128)(2,1)S(1)}, u32[]{:S(2)}, u32[]{:S(2)}) collective-permute-start(bf16[8,80,896]{2,1,0:T(8,128)(2,1)S(1)} %bitcast.57), channel_id=1, source_target_pairs={{0,192},{64,0},{128,64},{192,128},{1,193},{65,1},{129,65},{193,129... | collective-permute-start | bytes 3440648 | tf_op jit(solution)/shard_map/ppermute | solution.py:57
  438.5 23.3 %collective-permute-done.5 = bf16[8,80,896]{2,1,0:T(8,128)(2,1)S(1)} collective-permute-done((bf16[8,80,896]{2,1,0:T(8,128)(2,1)S(1)}, bf16[8,80,896]{2,1,0:T(8,128)(2,1)S(1)}, u32[]{:S(2)}, u32[]{:S(2)}) %collective-permute-start.5) | collective-permute-done | bytes 1146912 | tf_op jit(solution)/shard_map/ppermute | solution.py:57
  461.8 74.4 %collective-permute-done.4 = bf16[8,80,896]{2,1,0:T(8,128)(2,1)S(1)} collective-permute-done((bf16[8,80,896]{2,1,0:T(8,128)(2,1)S(1)}, bf16[8,80,896]{2,1,0:T(8,128)(2,1)S(1)}, u32[]{:S(2)}, u32[]{:S(2)}) %collective-permute-start.4) | collective-permute-done | bytes 1146912 | tf_op jit(solution)/shard_map/ppermute | solution.py:57
  538.8 5.8 all-to-all-start.1
  544.6 4.8 mini-gather-slice.2
  549.4 4.8 mini-gather-slice.3
  554.3 5.5 gather_fusion
  559.7 5.5 gather_fusion.1
  565.3 32.3 %all-to-all-done.1 = bf16[4,8,80,896]{3,2,0,1:T(8,128)(2,1)} async-done(((bf16[4,8,80,896]{3,2,0,1:T(8,128)(2,1)}), bf16[4,8,80,896]{3,2,0,1:T(8,128)(2,1)}, u32[]{:S(2)}, u32[]{:S(2)}) %all-to-all-start.1) | async-done | bytes 4587552 | tf_op jit(solution)/shard_map/all_to_all | solution.py:59
  597.6 8.9 %convert_reduce_fusion = (f32[80,1728]{1,0:T(8,128)S(1)}, f32[80,1728]{1,0:T(8,128)S(1)}) fusion(bf16[4,8,80,832]{3,2,1,0:T(8,128)(2,1)} %gather_fusion.1, bf16[4,8,80,896]{3,2,1,0:T(8,128)(2,1)} %gather_fusion, pred[4]{0:T(512)(128)(4,1)S(1)} %compare_and_fusion, bf16[4,8,80,832]{3,2,0,1:T(8,128)(2,1)} %all-to-all-done.3, ...), kind=kLoop, calls=%fused_computation.3 | loop fusion | flops 61655040 | bytes 18800644 | tf_op jit(solution)/shard_map/reduce_sum | solution.py:63
  (47 shorter events, 32.8 us)
Async XLA Ops:
  15.4 60.7 %all-to-all-start.2 = ((bf16[4,8,80,832]{3,2,0,1:T(8,128)(2,1)}), bf16[4,8,80,832]{3,2,0,1:T(8,128)(2,1)}, u32[]{:S(2)}, u32[]{:S(2)}) async-start(bf16[4,8,80,832]{3,2,0,1:T(8,128)(2,1)} %copy.26), calls=%async_computation.2 | async-start | bytes 9175040 | tf_op jit(solution)/shard_map/all_to_all | solution.py:42
  23.0 155.9 %all-gather.2.cloned.1.call-start = ((), (), s32[]{:S(2)}) async-start(), calls=%async_computation.4 | async-start | bytes 2949120 | tf_op jit(solution)/shard_map/all_gather | solution.py:30
  23.8 60.0 %slice-start.1 = ((f32[80,1728]{1,0:T(8,128)}), f32[80,896]{1,0:T(8,128)S(1)}, s32[]{:S(2)}) async-start(f32[80,1728]{1,0:T(8,128)} %param.7), calls=%async_computation.6 | async-start | bytes 573440 | tf_op jit(solution)/shard_map/slice | solution.py:38
  80.1 40.3 %collective-permute-start.8 = (bf16[8,80,832]{2,1,0:T(8,128)(2,1)}, bf16[8,80,832]{2,1,0:T(8,128)(2,1)}, u32[]{:S(2)}, u32[]{:S(2)}) collective-permute-start(bf16[8,80,832]{2,1,0:T(8,128)(2,1)} %get-tuple-element.15), channel_id=1, source_target_pairs={{0,64},{64,128},{128,192},{192,0},{1,65},{65,129},{129,193},{193,1... | collective-permute-start | bytes 3194888 | tf_op jit(solution)/shard_map/ppermute | solution.py:49
  80.1 93.9 %collective-permute-start.7 = (bf16[8,80,832]{2,1,0:T(8,128)(2,1)}, bf16[8,80,832]{2,1,0:T(8,128)(2,1)}, u32[]{:S(2)}, u32[]{:S(2)}) collective-permute-start(bf16[8,80,832]{2,1,0:T(8,128)(2,1)} %get-tuple-element.16), channel_id=1, source_target_pairs={{0,128},{64,192},{128,0},{192,64},{1,129},{65,193},{129,1},{193,65... | collective-permute-start | bytes 3194888 | tf_op jit(solution)/shard_map/ppermute | solution.py:49
  83.0 91.0 %collective-permute-start.6 = (bf16[8,80,832]{2,1,0:T(8,128)(2,1)S(1)}, bf16[8,80,832]{2,1,0:T(8,128)(2,1)}, u32[]{:S(2)}, u32[]{:S(2)}) collective-permute-start(bf16[8,80,832]{2,1,0:T(8,128)(2,1)S(1)} %get-tuple-element.17), channel_id=1, source_target_pairs={{0,192},{64,0},{128,64},{192,128},{1,193},{65,1},{129,65},{193,129... | collective-permute-start | bytes 3194888 | tf_op jit(solution)/shard_map/ppermute | solution.py:49
  89.8 135.9 %all-to-all-start = ((bf16[4,8,80,896]{3,2,0,1:T(8,128)(2,1)}), bf16[4,8,80,896]{3,2,0,1:T(8,128)(2,1)}, u32[]{:S(2)}, u32[]{:S(2)}) async-start(bf16[4,8,80,896]{3,2,0,1:T(8,128)(2,1)} %copy.22), calls=%async_computation | async-start | bytes 9175040 | tf_op jit(solution)/shard_map/all_to_all | solution.py:42
  176.4 2.6 copy-start
  195.5 49.6 %collective-permute-start.9 = (bf16[8,80,832]{2,1,0:T(8,128)(2,1)}, bf16[8,80,832]{2,1,0:T(8,128)(2,1)}, u32[]{:S(2)}, u32[]{:S(2)}) collective-permute-start(bf16[8,80,832]{2,1,0:T(8,128)(2,1)} %bitcast.60), channel_id=1, source_target_pairs={{0,64},{64,128},{128,192},{192,0},{1,65},{65,129},{129,193},{193,1... | collective-permute-start | bytes 3194888 | tf_op jit(solution)/shard_map/ppermute | solution.py:57
  223.7 72.2 %collective-permute-start.10 = (bf16[8,80,832]{2,1,0:T(8,128)(2,1)}, bf16[8,80,832]{2,1,0:T(8,128)(2,1)}, u32[]{:S(2)}, u32[]{:S(2)}) collective-permute-start(bf16[8,80,832]{2,1,0:T(8,128)(2,1)} %bitcast.27), channel_id=1, source_target_pairs={{0,128},{64,192},{128,0},{192,64},{1,129},{65,193},{129,1},{193,65... | collective-permute-start | bytes 3194888 | tf_op jit(solution)/shard_map/ppermute | solution.py:57
  223.7 72.2 %collective-permute-start.11 = (bf16[8,80,832]{2,1,0:T(8,128)(2,1)}, bf16[8,80,832]{2,1,0:T(8,128)(2,1)}, u32[]{:S(2)}, u32[]{:S(2)}) collective-permute-start(bf16[8,80,832]{2,1,0:T(8,128)(2,1)} %bitcast.59), channel_id=1, source_target_pairs={{0,192},{64,0},{128,64},{192,128},{1,193},{65,1},{129,65},{193,129... | collective-permute-start | bytes 3194888 | tf_op jit(solution)/shard_map/ppermute | solution.py:57
  230.0 88.9 %collective-permute-start.2 = (bf16[8,80,896]{2,1,0:T(8,128)(2,1)}, bf16[8,80,896]{2,1,0:T(8,128)(2,1)}, u32[]{:S(2)}, u32[]{:S(2)}) collective-permute-start(bf16[8,80,896]{2,1,0:T(8,128)(2,1)} %get-tuple-element.11), channel_id=1, source_target_pairs={{0,64},{64,128},{128,192},{192,0},{1,65},{65,129},{129,193},{193,1... | collective-permute-start | bytes 3440648 | tf_op jit(solution)/shard_map/ppermute | solution.py:49
  230.0 163.4 %collective-permute-start.1 = (bf16[8,80,896]{2,1,0:T(8,128)(2,1)}, bf16[8,80,896]{2,1,0:T(8,128)(2,1)}, u32[]{:S(2)}, u32[]{:S(2)}) collective-permute-start(bf16[8,80,896]{2,1,0:T(8,128)(2,1)} %get-tuple-element.12), channel_id=1, source_target_pairs={{0,128},{64,192},{128,0},{192,64},{1,129},{65,193},{129,1},{193,65... | collective-permute-start | bytes 3440648 | tf_op jit(solution)/shard_map/ppermute | solution.py:49
  245.1 148.3 %collective-permute-start = (bf16[8,80,896]{2,1,0:T(8,128)(2,1)}, bf16[8,80,896]{2,1,0:T(8,128)(2,1)}, u32[]{:S(2)}, u32[]{:S(2)}) collective-permute-start(bf16[8,80,896]{2,1,0:T(8,128)(2,1)} %get-tuple-element.13), channel_id=1, source_target_pairs={{0,192},{64,0},{128,64},{192,128},{1,193},{65,1},{129,65},{193,129... | collective-permute-start | bytes 3440648 | tf_op jit(solution)/shard_map/ppermute | solution.py:49
  300.8 5.3 slice-start
  300.8 238.0 %all-to-all-start.3 = ((bf16[4,8,80,832]{3,2,0,1:T(8,128)(2,1)}), bf16[4,8,80,832]{3,2,0,1:T(8,128)(2,1)}, u32[]{:S(2)}, u32[]{:S(2)}) async-start(bf16[4,8,80,832]{3,2,0,1:T(8,128)(2,1)} %copy.32), calls=%async_computation.3 | async-start | bytes 9175040 | tf_op jit(solution)/shard_map/all_to_all | solution.py:59
  411.5 50.3 %collective-permute-start.5 = (bf16[8,80,896]{2,1,0:T(8,128)(2,1)S(1)}, bf16[8,80,896]{2,1,0:T(8,128)(2,1)S(1)}, u32[]{:S(2)}, u32[]{:S(2)}) collective-permute-start(bf16[8,80,896]{2,1,0:T(8,128)(2,1)S(1)} %bitcast.57), channel_id=1, source_target_pairs={{0,192},{64,0},{128,64},{192,128},{1,193},{65,1},{129,65},{193,129... | collective-permute-start | bytes 3440648 | tf_op jit(solution)/shard_map/ppermute | solution.py:57
  438.1 98.1 %collective-permute-start.4 = (bf16[8,80,896]{2,1,0:T(8,128)(2,1)S(1)}, bf16[8,80,896]{2,1,0:T(8,128)(2,1)S(1)}, u32[]{:S(2)}, u32[]{:S(2)}) collective-permute-start(bf16[8,80,896]{2,1,0:T(8,128)(2,1)S(1)} %bitcast.55), channel_id=1, source_target_pairs={{0,128},{64,192},{128,0},{192,64},{1,129},{65,193},{129,1},{193,65... | collective-permute-start | bytes 3440648 | tf_op jit(solution)/shard_map/ppermute | solution.py:57
  438.1 98.1 %collective-permute-start.3 = (bf16[8,80,896]{2,1,0:T(8,128)(2,1)S(1)}, bf16[8,80,896]{2,1,0:T(8,128)(2,1)S(1)}, u32[]{:S(2)}, u32[]{:S(2)}) collective-permute-start(bf16[8,80,896]{2,1,0:T(8,128)(2,1)S(1)} %bitcast.53), channel_id=1, source_target_pairs={{0,64},{64,128},{128,192},{192,0},{1,65},{65,129},{129,193},{193,1... | collective-permute-start | bytes 3440648 | tf_op jit(solution)/shard_map/ppermute | solution.py:57
  538.8 58.9 %all-to-all-start.1 = ((bf16[4,8,80,896]{3,2,0,1:T(8,128)(2,1)}), bf16[4,8,80,896]{3,2,0,1:T(8,128)(2,1)}, u32[]{:S(2)}, u32[]{:S(2)}) async-start(bf16[4,8,80,896]{3,2,0,1:T(8,128)(2,1)} %pad_maximum_fusion.2), calls=%async_computation.1 | async-start | bytes 9175040 | tf_op jit(solution)/shard_map/all_to_all | solution.py:59
  565.3 41.3 %copy-start.1 = (f32[80,1728]{1,0:T(8,128)S(1)}, f32[80,1728]{1,0:T(8,128)}, u32[]{:S(2)}) copy-start(f32[80,1728]{1,0:T(8,128)} %param.7) | copy-start | bytes 1658884
  565.3 41.3 %copy-start.2 = (f32[80,1728]{1,0:T(8,128)S(1)}, f32[80,1728]{1,0:T(8,128)}, u32[]{:S(2)}) copy-start(f32[80,1728]{1,0:T(8,128)} %param.8) | copy-start | bytes 1658884
Sparse Core Ops, SparseCore 0:
  26.4 82.0 all-gather.1

commit v4 on v2

--- a/solution.py
+++ b/solution.py
@@ -20,36 +20,58 @@
     return [(0, first), (first, width)] if first < width else [(0, width)]
 
 
+def exchange_by_permutes(blocks, axis, n, me, outward):
+    got = [lax.dynamic_index_in_dim(blocks, me, axis=0, keepdims=False) if not outward else blocks[0]]
+    for d in range(1, n):
+        if outward:
+            part = blocks[d]
+            perm = [(i, (i + d) % n) for i in range(n)]
+        else:
+            part = lax.dynamic_index_in_dim(blocks, (me - d) % n, axis=0, keepdims=False)
+            perm = [(i, (i - d) % n) for i in range(n)]
+        got.append(lax.ppermute(part, axis, perm))
+    return jnp.stack(got)
+
+
 def local(tokens, target, post_mean, post_hess, weight_noise):
-    groups = weight_noise.shape[0]
+    groups, rows, width = weight_noise.shape
+    me = lax.axis_index("grp")
     post_std = lax.rsqrt(sample_size * (post_hess + weight_decay))
     group_x = lax.all_gather(tokens, "shard", axis=0, tiled=True)
-    chunks = column_chunks(weight_noise.shape[-1])
+    doubled = jnp.concatenate([group_x, group_x], axis=1)
+    x_r = lax.dynamic_slice_in_dim(doubled, me * rows, group_x.shape[1], axis=1)
+    chunks = column_chunks(width)
+    via_permutes = [i == len(chunks) - 1 and len(chunks) > 1 for i in range(len(chunks))]
     my_samples = []
-    for lo, hi in chunks:
+    for (lo, hi), perm_path in zip(chunks, via_permutes):
         noise_vals = weight_noise[:, :, lo:hi].astype(jnp.float32)
         samples = (post_mean[None, :, lo:hi] + post_std[None, :, lo:hi] * noise_vals).astype(
             jnp.bfloat16
         )
-        my_samples.append(lax.all_to_all(samples, "grp", split_axis=0, concat_axis=0, tiled=True))
-    grads = []
-    for (lo, hi), my_sample in zip(chunks, my_samples):
-        output = jnp.dot(
-            group_x,
-            my_sample.reshape(-1, hi - lo),
-            preferred_element_type=jnp.float32,
-        )
+        if perm_path:
+            my_samples.append(exchange_by_permutes(samples, "grp", groups, me, False))
+        else:
+            my_samples.append(
+                lax.all_to_all(samples, "grp", split_axis=0, concat_axis=0, tiled=True)
+            )
+    means, hesses = [], []
+    for (lo, hi), perm_path, my_sample in zip(chunks, via_permutes, my_samples):
+        xs = x_r if perm_path else group_x
+        output = jnp.dot(xs, my_sample.reshape(-1, hi - lo), preferred_element_type=jnp.float32)
         residual = (output - target[:, lo:hi].astype(jnp.float32)).astype(jnp.bfloat16)
-        gradient = contract_rows(group_x, residual).astype(jnp.bfloat16)
-        grads.append(
-            lax.all_to_all(
-                gradient.reshape(my_sample.shape), "grp", split_axis=0, concat_axis=0, tiled=True
-            )
-        )
-    group_grads = jnp.concatenate(grads, axis=-1).astype(jnp.float32)
-    noise_vals = weight_noise.astype(jnp.float32)
-    mean_grad = jnp.sum(group_grads, axis=0) / groups
-    hess_est = jnp.sum(group_grads * noise_vals, axis=0) / groups / post_std
+        gradient = contract_rows(xs, residual).astype(jnp.bfloat16).reshape(my_sample.shape)
+        noise_c = weight_noise[:, :, lo:hi]
+        if perm_path:
+            group_grads = exchange_by_permutes(gradient, "grp", groups, me, True)
+            order = (me - jnp.arange(groups)) % groups
+            noise_c = jnp.take(noise_c, order, axis=0)
+        else:
+            group_grads = lax.all_to_all(gradient, "grp", split_axis=0, concat_axis=0, tiled=True)
+        group_grads = group_grads.astype(jnp.float32)
+        means.append(jnp.sum(group_grads, axis=0))
+        hesses.append(jnp.sum(group_grads * noise_c.astype(jnp.float32), axis=0))
+    mean_grad = jnp.concatenate(means, axis=-1) / groups
+    hess_est = jnp.concatenate(hesses, axis=-1) / groups / post_std
     keep_rate = 1.0 - hess_decay
     gap = post_hess - hess_est
     new_hess = (

time: 505 us -> 816 us (1.62); the launches traced: 504 us -> 805 us
  starting transfers between devices: 23.5 us -> 262 us
  waiting for transfers between devices: 299 us -> 419 us
  blocking collectives: 110 us -> 0 us
  local copies, waits for them, and re-layouts: 15.4 us -> 64.8 us
    ppermute x0 -> x62, waiting for transfers between devices: none -> 419 us  [exchange_by_permutes(): got.append(lax.ppermute(part, axis, perm))]
    ppermute x0 -> x62, starting transfers between devices: none -> 250 us  [exchange_by_permutes(): got.append(lax.ppermute(part, axis, perm))]
    all_gather x1, waiting for transfers between devices: 110 us -> 0.01 us  [local(): group_x = lax.all_gather(tokens, 'shard', axis=0, tiled=True)]
    all_to_all x1 -> x0, blocking collectives: 110 us -> none  [local(): lax.all_to_all(gradient.reshape(my_sample.shape), 'grp', split_axis=0, co...]
    all_to_all x2 -> x1, waiting for transfers between devices: 103 us -> 0.01 us  [local(): lax.all_to_all(samples, 'grp', split_axis=0, concat_axis=0, tiled=True)]
    all_to_all x1, waiting for transfers between devices: 84.8 us -> 0.01 us  [local(): lax.all_to_all(gradient, 'grp', split_axis=0, concat_axis=0, tiled=True)]
    unnamed x6 -> x93, local copies, waits for them, and re-layouts: 0.01 us -> 25.9 us
    gather x0 -> x2, local copies, waits for them, and re-layouts: none -> 13.6 us  [local(): noise_c = jnp.take(noise_c, order, axis=0)]
  transfers between devices with their start and end apart: 4 -> 65, of which waited for: 4 -> 49; matrix products, arithmetic and copies ran while one was open for 8% -> 10% of each run, Pallas kernels for 0% -> 0%
where the time goes in v4:
time: 816 us; the launch traced here: 805 us
  waiting for transfers between devices  419 us (51%)
  starting transfers between devices  262 us (32%)
  local copies, waits for them, and re-layouts  64.8 us (8%)
  matrix products  21.8 us (3%)
  other arithmetic  20.9 us (3%)
  between operations  15.4 us (2%)
    ppermute x62, waiting for transfers between devices, exchange_by_permutes(): got.append(lax.ppermute(part, axis, perm))  419 us
    ppermute x62, starting transfers between devices, exchange_by_permutes(): got.append(lax.ppermute(part, axis, perm))  250 us
    unnamed x93, local copies, waits for them, and re-layouts  25.9 us
    dot_general x2, matrix products, contract_rows(): lax.dot_general(left, right, (((0,), (0,)), ((), ())), preferred_element_...  21.8 us
  transfers between devices with their start and end apart: 65, of which 49 were waited for; matrix products, arithmetic and copies ran while one was open for 10% of the time, Pallas kernels for 0%

profile of v4, /device:TPU:1, one launch (start us, length us, event | category | flops | bytes accessed | tf_op | source)
XLA Modules:
  0.0 804.7 jit_solution(12295261617008118555)
XLA Ops:
  34.1 7.7 all-to-all-start
  52.2 8.1 %copy.12 = bf16[32,80,832]{1,2,0:T(8,128)(2,1)} copy(bf16[32,80,832]{2,1,0:T(8,128)(2,1)} %gather_fusion) | data formatting | bytes 8519680 | tf_op jit(solution)/shard_map/jit(_take)/gather | solution.py:67
  67.5 81.2 %collective-permute-done.1 = bf16[80,832]{1,0:T(8,128)(2,1)S(1)} collective-permute-done((bf16[80,832]{1,0:T(8,128)(2,1)S(1)}, bf16[80,832]{1,0:T(8,128)(2,1)S(1)}, u32[]{:S(2)}, u32[]{:S(2)}) %collective-permute-start.1) | collective-permute-done | bytes 133152 | tf_op jit(solution)/shard_map/ppermute | solution.py:32
  148.7 9.1 %collective-permute-start.2 = (bf16[80,832]{1,0:T(8,128)(2,1)S(1)}, bf16[80,832]{1,0:T(8,128)(2,1)S(1)}, u32[]{:S(2)}, u32[]{:S(2)}) collective-permute-start(bf16[80,832]{1,0:T(8,128)(2,1)S(1)} %get-tuple-element.36), channel_id=1, source_target_pairs={{0,232},{8,240},{16,248},{24,0},{32,8},{40,16},{48,24},{56,32},{64... | collective-permute-start | bytes 399368 | tf_op jit(solution)/shard_map/ppermute | solution.py:32
  166.3 16.3 %collective-permute-start.4 = (bf16[80,832]{1,0:T(8,128)(2,1)S(1)}, bf16[80,832]{1,0:T(8,128)(2,1)S(1)}, u32[]{:S(2)}, u32[]{:S(2)}) collective-permute-start(bf16[80,832]{1,0:T(8,128)(2,1)S(1)} %get-tuple-element.34), channel_id=1, source_target_pairs={{0,216},{8,224},{16,232},{24,240},{32,248},{40,0},{48,8},{56,16},{... | collective-permute-start | bytes 399368 | tf_op jit(solution)/shard_map/ppermute | solution.py:32
  185.5 17.1 %collective-permute-start.5 = (bf16[80,832]{1,0:T(8,128)(2,1)S(1)}, bf16[80,832]{1,0:T(8,128)(2,1)S(1)}, u32[]{:S(2)}, u32[]{:S(2)}) collective-permute-start(bf16[80,832]{1,0:T(8,128)(2,1)S(1)} %get-tuple-element.33), channel_id=1, source_target_pairs={{0,208},{8,216},{16,224},{24,232},{32,240},{40,248},{48,0},{56,8},... | collective-permute-start | bytes 399368 | tf_op jit(solution)/shard_map/ppermute | solution.py:32
  314.8 7.7 collective-permute-start.19
  344.1 11.7 %collective-permute-done.22 = bf16[80,832]{1,0:T(8,128)(2,1)S(1)} collective-permute-done((bf16[80,832]{1,0:T(8,128)(2,1)S(1)}, bf16[80,832]{1,0:T(8,128)(2,1)S(1)}, u32[]{:S(2)}, u32[]{:S(2)}) %collective-permute-start.22) | collective-permute-done | bytes 133152 | tf_op jit(solution)/shard_map/ppermute | solution.py:32
  362.2 7.7 collective-permute-done.24
  370.6 7.2 collective-permute-done.25
  379.0 8.8 %collective-permute-done.26 = bf16[80,832]{1,0:T(8,128)(2,1)S(1)} collective-permute-done((bf16[80,832]{1,0:T(8,128)(2,1)S(1)}, bf16[80,832]{1,0:T(8,128)(2,1)S(1)}, u32[]{:S(2)}, u32[]{:S(2)}) %collective-permute-start.26) | collective-permute-done | bytes 133152 | tf_op jit(solution)/shard_map/ppermute | solution.py:32
  392.1 12.2 %convolution_convert_fusion.1 = bf16[2560,832]{0,1:T(8,128)(2,1)} fusion(bf16[2560,832]{1,0:T(8,128)(2,1)} %bitcast.210, bf16[512,1728]{0,1:T(8,128)(2,1)} %param.6, s32[]{:T(128)S(6)} %select_n.264, bf16[512,2560]{1,0:T(8,128)(2,1)} %all-gather.2.cloned.1.call-done), kind=kOutput, calls=%fused_computation.14 | convolution fusion | flops 4375969792 | bytes 14943232 | tf_op jit(solution)/shard_map/dot_general | solution.py:13
  404.3 9.6 %fusion.4 = bf16[2560,896]{0,1:T(8,128)(2,1)} fusion(bf16[512,2560]{1,0:T(8,128)(2,1)S(1)} %copy-done.13, bf16[2560,896]{1,0:T(8,128)(2,1)} %bitcast, bf16[512,1728]{0,1:T(8,128)(2,1)} %param.6), kind=kOutput, calls=%fused_computation.15 | convolution fusion | flops 4701290496 | bytes 15335424 | tf_op jit(solution)/shard_map/dot_general | solution.py:13
  413.9 7.2 copy.10
  442.2 12.2 %collective-permute-done.31 = bf16[80,832]{0,1:T(8,128)(2,1)S(1)} collective-permute-done((bf16[80,832]{0,1:T(8,128)(2,1)S(1)}, bf16[80,832]{0,1:T(8,128)(2,1)S(1)}, u32[]{:S(2)}, u32[]{:S(2)}) %collective-permute-start.31) | collective-permute-done | bytes 133152 | tf_op jit(solution)/shard_map/ppermute | solution.py:32
  454.9 75.0 %collective-permute-done.32 = bf16[80,832]{0,1:T(8,128)(2,1)S(1)} collective-permute-done((bf16[80,832]{0,1:T(8,128)(2,1)S(1)}, bf16[80,832]{0,1:T(8,128)(2,1)S(1)}, u32[]{:S(2)}, u32[]{:S(2)}) %collective-permute-start.32) | collective-permute-done | bytes 133152 | tf_op jit(solution)/shard_map/ppermute | solution.py:32
  530.0 11.5 %collective-permute-done.33 = bf16[80,832]{0,1:T(8,128)(2,1)S(1)} collective-permute-done((bf16[80,832]{0,1:T(8,128)(2,1)S(1)}, bf16[80,832]{0,1:T(8,128)(2,1)S(1)}, u32[]{:S(2)}, u32[]{:S(2)}) %collective-permute-start.33) | collective-permute-done | bytes 133152 | tf_op jit(solution)/shard_map/ppermute | solution.py:32
  550.5 27.8 %collective-permute-start.35 = (bf16[80,832]{0,1:T(8,128)(2,1)S(1)}, bf16[80,832]{0,1:T(8,128)(2,1)S(1)}, u32[]{:S(2)}, u32[]{:S(2)}) collective-permute-start(bf16[80,832]{0,1:T(8,128)(2,1)S(1)} %get-tuple-element.66), channel_id=1, source_target_pairs={{0,40},{8,48},{16,56},{24,64},{32,72},{40,80},{48,88},{56,96},{64,... | collective-permute-start | bytes 399368 | tf_op jit(solution)/shard_map/ppermute | solution.py:32
  581.1 12.1 %collective-permute-start.36 = (bf16[80,832]{0,1:T(8,128)(2,1)S(1)}, bf16[80,832]{0,1:T(8,128)(2,1)S(1)}, u32[]{:S(2)}, u32[]{:S(2)}) collective-permute-start(bf16[80,832]{0,1:T(8,128)(2,1)S(1)} %get-tuple-element.65), channel_id=1, source_target_pairs={{0,48},{8,56},{16,64},{24,72},{32,80},{40,88},{48,96},{56,104},{64... | collective-permute-start | bytes 399368 | tf_op jit(solution)/shard_map/ppermute | solution.py:32
  601.7 6.8 collective-permute-done.37
  608.5 9.6 %collective-permute-done.38 = bf16[80,832]{0,1:T(8,128)(2,1)S(1)} collective-permute-done((bf16[80,832]{0,1:T(8,128)(2,1)S(1)}, bf16[80,832]{0,1:T(8,128)(2,1)S(1)}, u32[]{:S(2)}, u32[]{:S(2)}) %collective-permute-start.38) | collective-permute-done | bytes 133152 | tf_op jit(solution)/shard_map/ppermute | solution.py:32
  625.4 18.9 %collective-permute-done.43 = bf16[80,832]{0,1:T(8,128)(2,1)S(1)} collective-permute-done((bf16[80,832]{0,1:T(8,128)(2,1)S(1)}, bf16[80,832]{0,1:T(8,128)(2,1)S(1)}, u32[]{:S(2)}, u32[]{:S(2)}) %collective-permute-start.43) | collective-permute-done | bytes 133152 | tf_op jit(solution)/shard_map/ppermute | solution.py:32
  650.8 7.0 collective-permute-start.45
  657.9 6.9 collective-permute-done.45
  664.9 9.7 %collective-permute-done.46 = bf16[80,832]{0,1:T(8,128)(2,1)S(1)} collective-permute-done((bf16[80,832]{0,1:T(8,128)(2,1)S(1)}, bf16[80,832]{0,1:T(8,128)(2,1)S(1)}, u32[]{:S(2)}, u32[]{:S(2)}) %collective-permute-start.46) | collective-permute-done | bytes 133152 | tf_op jit(solution)/shard_map/ppermute | solution.py:32
  677.6 7.3 collective-permute-done.47
  684.9 8.5 %collective-permute-done.48 = bf16[80,832]{0,1:T(8,128)(2,1)S(1)} collective-permute-done((bf16[80,832]{0,1:T(8,128)(2,1)S(1)}, bf16[80,832]{0,1:T(8,128)(2,1)S(1)}, u32[]{:S(2)}, u32[]{:S(2)}) %collective-permute-start.48) | collective-permute-done | bytes 133152 | tf_op jit(solution)/shard_map/ppermute | solution.py:32
  711.2 7.1 collective-permute-start.51
  718.3 7.6 collective-permute-done.51
  733.2 6.9 collective-permute-start.53
  743.1 7.6 collective-permute-start.54
  760.8 8.1 %collective-permute-done.55 = bf16[80,832]{0,1:T(8,128)(2,1)S(1)} collective-permute-done((bf16[80,832]{0,1:T(8,128)(2,1)S(1)}, bf16[80,832]{0,1:T(8,128)(2,1)S(1)}, u32[]{:S(2)}, u32[]{:S(2)}) %collective-permute-start.55) | collective-permute-done | bytes 133152 | tf_op jit(solution)/shard_map/ppermute | solution.py:32
  (221 shorter events, 327.1 us)
Async XLA Ops:
  7.2 384.9 %all-gather.2.cloned.1.call-start = ((), (), s32[]{:S(2)}) async-start(), calls=%async_computation.2 | async-start | bytes 2949120 | tf_op jit(solution)/shard_map/all_gather | solution.py:40
  17.6 373.8 %collective-permute-start.30 = (bf16[80,832]{1,0:T(8,128)(2,1)}, bf16[80,832]{1,0:T(8,128)(2,1)S(1)}, u32[]{:S(2)}, u32[]{:S(2)}) collective-permute-start(bf16[80,832]{1,0:T(8,128)(2,1)} %get-tuple-element.8), channel_id=1, source_target_pairs={{0,8},{8,16},{16,24},{24,32},{32,40},{40,48},{48,56},{56,64},{64,7... | collective-permute-start | bytes 399368 | tf_op jit(solution)/shard_map/ppermute | solution.py:32
  20.2 370.6 %collective-permute-start.29 = (bf16[80,832]{1,0:T(8,128)(2,1)}, bf16[80,832]{1,0:T(8,128)(2,1)S(1)}, u32[]{:S(2)}, u32[]{:S(2)}) collective-permute-start(bf16[80,832]{1,0:T(8,128)(2,1)} %get-tuple-element.9), channel_id=1, source_target_pairs={{0,16},{8,24},{16,32},{24,40},{32,48},{40,56},{48,64},{56,72},{64,... | collective-permute-start | bytes 399368 | tf_op jit(solution)/shard_map/ppermute | solution.py:32
  21.4 368.7 %collective-permute-start.28 = (bf16[80,832]{1,0:T(8,128)(2,1)}, bf16[80,832]{1,0:T(8,128)(2,1)S(1)}, u32[]{:S(2)}, u32[]{:S(2)}) collective-permute-start(bf16[80,832]{1,0:T(8,128)(2,1)} %get-tuple-element.10), channel_id=1, source_target_pairs={{0,24},{8,32},{16,40},{24,48},{32,56},{40,64},{48,72},{56,80},{64,... | collective-permute-start | bytes 399368 | tf_op jit(solution)/shard_map/ppermute | solution.py:32
  23.0 365.5 %collective-permute-start.27 = (bf16[80,832]{1,0:T(8,128)(2,1)}, bf16[80,832]{1,0:T(8,128)(2,1)}, u32[]{:S(2)}, u32[]{:S(2)}) collective-permute-start(bf16[80,832]{1,0:T(8,128)(2,1)} %get-tuple-element.11), channel_id=1, source_target_pairs={{0,32},{8,40},{16,48},{24,56},{32,64},{40,72},{48,80},{56,88},{64,... | collective-permute-start | bytes 399368 | tf_op jit(solution)/shard_map/ppermute | solution.py:32
  27.3 33.1 %collective-permute-start = (bf16[80,832]{1,0:T(8,128)(2,1)S(1)}, bf16[80,832]{1,0:T(8,128)(2,1)}, u32[]{:S(2)}, u32[]{:S(2)}) collective-permute-start(bf16[80,832]{1,0:T(8,128)(2,1)S(1)} %get-tuple-element.38), channel_id=1, source_target_pairs={{0,248},{8,0},{16,8},{24,16},{32,24},{40,32},{48,40},{56,48},{64,5... | collective-permute-start | bytes 399368 | tf_op jit(solution)/shard_map/ppermute | solution.py:32
  34.1 370.2 %all-to-all-start = ((bf16[32,80,896]{2,1,0:T(8,128)(2,1)}), bf16[32,80,896]{2,1,0:T(8,128)(2,1)}, u32[]{:S(2)}, u32[]{:S(2)}) async-start(bf16[32,80,896]{2,1,0:T(8,128)(2,1)} %fusion.2), calls=%async_computation | async-start | bytes 9175040 | tf_op jit(solution)/shard_map/all_to_all | solution.py:55
  60.4 88.3 %collective-permute-start.1 = (bf16[80,832]{1,0:T(8,128)(2,1)S(1)}, bf16[80,832]{1,0:T(8,128)(2,1)S(1)}, u32[]{:S(2)}, u32[]{:S(2)}) collective-permute-start(bf16[80,832]{1,0:T(8,128)(2,1)S(1)} %get-tuple-element.37), channel_id=1, source_target_pairs={{0,240},{8,248},{16,0},{24,8},{32,16},{40,24},{48,32},{56,40},{64,... | collective-permute-start | bytes 399368 | tf_op jit(solution)/shard_map/ppermute | solution.py:32
  148.7 11.2 %collective-permute-start.2 = (bf16[80,832]{1,0:T(8,128)(2,1)S(1)}, bf16[80,832]{1,0:T(8,128)(2,1)S(1)}, u32[]{:S(2)}, u32[]{:S(2)}) collective-permute-start(bf16[80,832]{1,0:T(8,128)(2,1)S(1)} %get-tuple-element.36), channel_id=1, source_target_pairs={{0,232},{8,240},{16,248},{24,0},{32,8},{40,16},{48,24},{56,32},{64... | collective-permute-start | bytes 399368 | tf_op jit(solution)/shard_map/ppermute | solution.py:32
  166.3 19.2 %collective-permute-start.4 = (bf16[80,832]{1,0:T(8,128)(2,1)S(1)}, bf16[80,832]{1,0:T(8,128)(2,1)S(1)}, u32[]{:S(2)}, u32[]{:S(2)}) collective-permute-start(bf16[80,832]{1,0:T(8,128)(2,1)S(1)} %get-tuple-element.34), channel_id=1, source_target_pairs={{0,216},{8,224},{16,232},{24,240},{32,248},{40,0},{48,8},{56,16},{... | collective-permute-start | bytes 399368 | tf_op jit(solution)/shard_map/ppermute | solution.py:32
  185.5 20.8 %collective-permute-start.5 = (bf16[80,832]{1,0:T(8,128)(2,1)S(1)}, bf16[80,832]{1,0:T(8,128)(2,1)S(1)}, u32[]{:S(2)}, u32[]{:S(2)}) collective-permute-start(bf16[80,832]{1,0:T(8,128)(2,1)S(1)} %get-tuple-element.33), channel_id=1, source_target_pairs={{0,208},{8,216},{16,224},{24,232},{32,240},{40,248},{48,0},{56,8},... | collective-permute-start | bytes 399368 | tf_op jit(solution)/shard_map/ppermute | solution.py:32
  206.3 12.5 %collective-permute-start.6 = (bf16[80,832]{1,0:T(8,128)(2,1)S(1)}, bf16[80,832]{1,0:T(8,128)(2,1)S(1)}, u32[]{:S(2)}, u32[]{:S(2)}) collective-permute-start(bf16[80,832]{1,0:T(8,128)(2,1)S(1)} %get-tuple-element.32), channel_id=1, source_target_pairs={{0,200},{8,208},{16,216},{24,224},{32,232},{40,240},{48,248},{56,0... | collective-permute-start | bytes 399368 | tf_op jit(solution)/shard_map/ppermute | solution.py:32
  341.8 14.0 %collective-permute-start.22 = (bf16[80,832]{1,0:T(8,128)(2,1)S(1)}, bf16[80,832]{1,0:T(8,128)(2,1)S(1)}, u32[]{:S(2)}, u32[]{:S(2)}) collective-permute-start(bf16[80,832]{1,0:T(8,128)(2,1)S(1)} %copy-done.7), channel_id=1, source_target_pairs={{0,72},{8,80},{16,88},{24,96},{32,104},{40,112},{48,120},{56,128},... | collective-permute-start | bytes 399368 | tf_op jit(solution)/shard_map/ppermute | solution.py:32
  421.1 369.4 %all-to-all-start.1 = ((bf16[32,80,896]{2,1,0:T(8,128)(2,1)}), bf16[32,80,896]{2,1,0:T(8,128)(2,1)}, u32[]{:S(2)}, u32[]{:S(2)}) async-start(bf16[32,80,896]{2,1,0:T(8,128)(2,1)} %bitcast.209), calls=%async_computation.1 | async-start | bytes 9175040 | tf_op jit(solution)/shard_map/all_to_all | solution.py:69
  429.0 192.8 %collective-permute-start.42 = (bf16[80,832]{0,1:T(8,128)(2,1)S(1)}, bf16[80,832]{0,1:T(8,128)(2,1)S(1)}, u32[]{:S(2)}, u32[]{:S(2)}) collective-permute-start(bf16[80,832]{0,1:T(8,128)(2,1)S(1)} %get-tuple-element.59), channel_id=1, source_target_pairs={{0,96},{8,104},{16,112},{24,120},{32,128},{40,136},{48,144},{56,15... | collective-permute-start | bytes 399368 | tf_op jit(solution)/shard_map/ppermute | solution.py:32
  431.5 189.8 %collective-permute-start.41 = (bf16[80,832]{0,1:T(8,128)(2,1)S(1)}, bf16[80,832]{0,1:T(8,128)(2,1)S(1)}, u32[]{:S(2)}, u32[]{:S(2)}) collective-permute-start(bf16[80,832]{0,1:T(8,128)(2,1)S(1)} %get-tuple-element.60), channel_id=1, source_target_pairs={{0,88},{8,96},{16,104},{24,112},{32,120},{40,128},{48,136},{56,144... | collective-permute-start | bytes 399368 | tf_op jit(solution)/shard_map/ppermute | solution.py:32
  434.2 184.9 %collective-permute-start.40 = (bf16[80,832]{0,1:T(8,128)(2,1)S(1)}, bf16[80,832]{0,1:T(8,128)(2,1)S(1)}, u32[]{:S(2)}, u32[]{:S(2)}) collective-permute-start(bf16[80,832]{0,1:T(8,128)(2,1)S(1)} %get-tuple-element.61), channel_id=1, source_target_pairs={{0,80},{8,88},{16,96},{24,104},{32,112},{40,120},{48,128},{56,136}... | collective-permute-start | bytes 399368 | tf_op jit(solution)/shard_map/ppermute | solution.py:32
  434.4 184.4 %collective-permute-start.39 = (bf16[80,832]{0,1:T(8,128)(2,1)S(1)}, bf16[80,832]{0,1:T(8,128)(2,1)S(1)}, u32[]{:S(2)}, u32[]{:S(2)}) collective-permute-start(bf16[80,832]{0,1:T(8,128)(2,1)S(1)} %get-tuple-element.62), channel_id=1, source_target_pairs={{0,72},{8,80},{16,88},{24,96},{32,104},{40,112},{48,120},{56,128},... | collective-permute-start | bytes 399368 | tf_op jit(solution)/shard_map/ppermute | solution.py:32
  435.6 18.8 %collective-permute-start.31 = (bf16[80,832]{0,1:T(8,128)(2,1)S(1)}, bf16[80,832]{0,1:T(8,128)(2,1)S(1)}, u32[]{:S(2)}, u32[]{:S(2)}) collective-permute-start(bf16[80,832]{0,1:T(8,128)(2,1)S(1)} %get-tuple-element.70), channel_id=1, source_target_pairs={{0,8},{8,16},{16,24},{24,32},{32,40},{40,48},{48,56},{56,64},{64,7... | collective-permute-start | bytes 399368 | tf_op jit(solution)/shard_map/ppermute | solution.py:32
  454.4 75.5 %collective-permute-start.32 = (bf16[80,832]{0,1:T(8,128)(2,1)S(1)}, bf16[80,832]{0,1:T(8,128)(2,1)S(1)}, u32[]{:S(2)}, u32[]{:S(2)}) collective-permute-start(bf16[80,832]{0,1:T(8,128)(2,1)S(1)} %get-tuple-element.69), channel_id=1, source_target_pairs={{0,16},{8,24},{16,32},{24,40},{32,48},{40,56},{48,64},{56,72},{64,... | collective-permute-start | bytes 399368 | tf_op jit(solution)/shard_map/ppermute | solution.py:32
  529.9 11.6 %collective-permute-start.33 = (bf16[80,832]{0,1:T(8,128)(2,1)S(1)}, bf16[80,832]{0,1:T(8,128)(2,1)S(1)}, u32[]{:S(2)}, u32[]{:S(2)}) collective-permute-start(bf16[80,832]{0,1:T(8,128)(2,1)S(1)} %get-tuple-element.68), channel_id=1, source_target_pairs={{0,24},{8,32},{16,40},{24,48},{32,56},{40,64},{48,72},{56,80},{64,... | collective-permute-start | bytes 399368 | tf_op jit(solution)/shard_map/ppermute | solution.py:32
  550.5 30.6 %collective-permute-start.35 = (bf16[80,832]{0,1:T(8,128)(2,1)S(1)}, bf16[80,832]{0,1:T(8,128)(2,1)S(1)}, u32[]{:S(2)}, u32[]{:S(2)}) collective-permute-start(bf16[80,832]{0,1:T(8,128)(2,1)S(1)} %get-tuple-element.66), channel_id=1, source_target_pairs={{0,40},{8,48},{16,56},{24,64},{32,72},{40,80},{48,88},{56,96},{64,... | collective-permute-start | bytes 399368 | tf_op jit(solution)/shard_map/ppermute | solution.py:32
  581.1 16.6 %collective-permute-start.36 = (bf16[80,832]{0,1:T(8,128)(2,1)S(1)}, bf16[80,832]{0,1:T(8,128)(2,1)S(1)}, u32[]{:S(2)}, u32[]{:S(2)}) collective-permute-start(bf16[80,832]{0,1:T(8,128)(2,1)S(1)} %get-tuple-element.65), channel_id=1, source_target_pairs={{0,48},{8,56},{16,64},{24,72},{32,80},{40,88},{48,96},{56,104},{64... | collective-permute-start | bytes 399368 | tf_op jit(solution)/shard_map/ppermute | solution.py:32
  618.2 168.0 %collective-permute-start.61 = (bf16[80,832]{0,1:T(8,128)(2,1)S(1)}, bf16[80,832]{0,1:T(8,128)(2,1)S(1)}, u32[]{:S(2)}, u32[]{:S(2)}) collective-permute-start(bf16[80,832]{0,1:T(8,128)(2,1)S(1)} %get-tuple-element.40), channel_id=1, source_target_pairs={{0,248},{8,0},{16,8},{24,16},{32,24},{40,32},{48,40},{56,48},{64,5... | collective-permute-start | bytes 399368 | tf_op jit(solution)/shard_map/ppermute | solution.py:32
  618.8 167.4 %collective-permute-start.60 = (bf16[80,832]{0,1:T(8,128)(2,1)S(1)}, bf16[80,832]{0,1:T(8,128)(2,1)S(1)}, u32[]{:S(2)}, u32[]{:S(2)}) collective-permute-start(bf16[80,832]{0,1:T(8,128)(2,1)S(1)} %get-tuple-element.41), channel_id=1, source_target_pairs={{0,240},{8,248},{16,0},{24,8},{32,16},{40,24},{48,32},{56,40},{64,... | collective-permute-start | bytes 399368 | tf_op jit(solution)/shard_map/ppermute | solution.py:32
  619.2 166.9 %collective-permute-start.59 = (bf16[80,832]{0,1:T(8,128)(2,1)S(1)}, bf16[80,832]{0,1:T(8,128)(2,1)S(1)}, u32[]{:S(2)}, u32[]{:S(2)}) collective-permute-start(bf16[80,832]{0,1:T(8,128)(2,1)S(1)} %get-tuple-element.42), channel_id=1, source_target_pairs={{0,232},{8,240},{16,248},{24,0},{32,8},{40,16},{48,24},{56,32},{64... | collective-permute-start | bytes 399368 | tf_op jit(solution)/shard_map/ppermute | solution.py:32
  621.3 164.8 %collective-permute-start.58 = (bf16[80,832]{0,1:T(8,128)(2,1)S(1)}, bf16[80,832]{0,1:T(8,128)(2,1)S(1)}, u32[]{:S(2)}, u32[]{:S(2)}) collective-permute-start(bf16[80,832]{0,1:T(8,128)(2,1)S(1)} %get-tuple-element.43), channel_id=1, source_target_pairs={{0,224},{8,232},{16,240},{24,248},{32,0},{40,8},{48,16},{56,24},{6... | collective-permute-start | bytes 399368 | tf_op jit(solution)/shard_map/ppermute | solution.py:32
  621.9 22.4 %collective-permute-start.43 = (bf16[80,832]{0,1:T(8,128)(2,1)S(1)}, bf16[80,832]{0,1:T(8,128)(2,1)S(1)}, u32[]{:S(2)}, u32[]{:S(2)}) collective-permute-start(bf16[80,832]{0,1:T(8,128)(2,1)S(1)} %get-tuple-element.58), channel_id=1, source_target_pairs={{0,104},{8,112},{16,120},{24,128},{32,136},{40,144},{48,152},{56,1... | collective-permute-start | bytes 399368 | tf_op jit(solution)/shard_map/ppermute | solution.py:32
  650.8 13.9 %collective-permute-start.45 = (bf16[80,832]{0,1:T(8,128)(2,1)S(1)}, bf16[80,832]{0,1:T(8,128)(2,1)S(1)}, u32[]{:S(2)}, u32[]{:S(2)}) collective-permute-start(bf16[80,832]{0,1:T(8,128)(2,1)S(1)} %get-tuple-element.56), channel_id=1, source_target_pairs={{0,120},{8,128},{16,136},{24,144},{32,152},{40,160},{48,168},{56,1... | collective-permute-start | bytes 399368 | tf_op jit(solution)/shard_map/ppermute | solution.py:32
  711.2 14.7 %collective-permute-start.51 = (bf16[80,832]{0,1:T(8,128)(2,1)S(1)}, bf16[80,832]{0,1:T(8,128)(2,1)S(1)}, u32[]{:S(2)}, u32[]{:S(2)}) collective-permute-start(bf16[80,832]{0,1:T(8,128)(2,1)S(1)} %get-tuple-element.50), channel_id=1, source_target_pairs={{0,168},{8,176},{16,184},{24,192},{32,200},{40,208},{48,216},{56,2... | collective-permute-start | bytes 399368 | tf_op jit(solution)/shard_map/ppermute | solution.py:32
  743.1 11.7 %collective-permute-start.54 = (bf16[80,832]{0,1:T(8,128)(2,1)S(1)}, bf16[80,832]{0,1:T(8,128)(2,1)S(1)}, u32[]{:S(2)}, u32[]{:S(2)}) collective-permute-start(bf16[80,832]{0,1:T(8,128)(2,1)S(1)} %get-tuple-element.47), channel_id=1, source_target_pairs={{0,192},{8,200},{16,208},{24,216},{32,224},{40,232},{48,240},{56,2... | collective-permute-start | bytes 399368 | tf_op jit(solution)/shard_map/ppermute | solution.py:32
  754.8 14.1 %collective-permute-start.55 = (bf16[80,832]{0,1:T(8,128)(2,1)S(1)}, bf16[80,832]{0,1:T(8,128)(2,1)S(1)}, u32[]{:S(2)}, u32[]{:S(2)}) collective-permute-start(bf16[80,832]{0,1:T(8,128)(2,1)S(1)} %get-tuple-element.46), channel_id=1, source_target_pairs={{0,200},{8,208},{16,216},{24,224},{32,232},{40,240},{48,248},{56,0... | collective-permute-start | bytes 399368 | tf_op jit(solution)/shard_map/ppermute | solution.py:32
  (50 other events, 3636.7 us)
Sparse Core Ops, SparseCore 0:
  10.6 100.4 all-gather.1

commit v5 on v2

--- a/solution.py
+++ b/solution.py
@@ -32,7 +32,7 @@
             jnp.bfloat16
         )
         my_samples.append(lax.all_to_all(samples, "grp", split_axis=0, concat_axis=0, tiled=True))
-    grads = []
+    means, hesses = [], []
     for (lo, hi), my_sample in zip(chunks, my_samples):
         output = jnp.dot(
             group_x,
@@ -41,25 +41,29 @@
         )
         residual = (output - target[:, lo:hi].astype(jnp.float32)).astype(jnp.bfloat16)
         gradient = contract_rows(group_x, residual).astype(jnp.bfloat16)
-        grads.append(
-            lax.all_to_all(
-                gradient.reshape(my_sample.shape), "grp", split_axis=0, concat_axis=0, tiled=True
-            )
+        group_grads = lax.all_to_all(
+            gradient.reshape(my_sample.shape), "grp", split_axis=0, concat_axis=0, tiled=True
+        ).astype(jnp.float32)
+        pm = post_mean[:, lo:hi]
+        ph = post_hess[:, lo:hi]
+        mean_grad = jnp.sum(group_grads, axis=0) / groups
+        hess_est = (
+            jnp.sum(group_grads * weight_noise[:, :, lo:hi].astype(jnp.float32), axis=0)
+            / groups
+            / post_std[:, lo:hi]
         )
-    group_grads = jnp.concatenate(grads, axis=-1).astype(jnp.float32)
-    noise_vals = weight_noise.astype(jnp.float32)
-    mean_grad = jnp.sum(group_grads, axis=0) / groups
-    hess_est = jnp.sum(group_grads * noise_vals, axis=0) / groups / post_std
-    keep_rate = 1.0 - hess_decay
-    gap = post_hess - hess_est
-    new_hess = (
-        hess_decay * post_hess
-        + keep_rate * hess_est
-        + 0.5 * keep_rate * keep_rate * gap * gap / (post_hess + weight_decay)
-    )
-    new_mean = post_mean - learn_rate * (mean_grad + weight_decay * post_mean) / (
-        new_hess + weight_decay
-    )
+        keep_rate = 1.0 - hess_decay
+        gap = ph - hess_est
+        new_hess = (
+            hess_decay * ph
+            + keep_rate * hess_est
+            + 0.5 * keep_rate * keep_rate * gap * gap / (ph + weight_decay)
+        )
+        new_mean = pm - learn_rate * (mean_grad + weight_decay * pm) / (new_hess + weight_decay)
+        means.append(new_mean)
+        hesses.append(new_hess)
+    new_mean = jnp.concatenate(means, axis=-1)
+    new_hess = jnp.concatenate(hesses, axis=-1)
     return (new_mean, new_hess)
 
 

time: 505 us -> 501 us (level)
  blocking collectives: 110 us -> 0 us
  waiting for transfers between devices: 299 us -> 395 us
  starting transfers between devices: 23.5 us -> 30.1 us
    all_to_all x1 -> x0, blocking collectives: 110 us -> none  [local(): lax.all_to_all(gradient.reshape(my_sample.shape), 'grp', split_axis=0, co...]
    all_to_all x1 -> x2, waiting for transfers between devices: 84.8 us -> 181 us  [local(): lax.all_to_all(gradient.reshape(my_sample.shape), 'grp', split_axis=0, co...]
    all_to_all x1 -> x2, starting transfers between devices: 6.65 us -> 13.3 us  [local(): lax.all_to_all(gradient.reshape(my_sample.shape), 'grp', split_axis=0, co...]
    reduce_sum x1 -> x2, other arithmetic: 7.6 us -> 11 us  [local(): mean_grad = jnp.sum(group_grads, axis=0) / groups]
  transfers between devices with their start and end apart: 4 -> 5, of which waited for: 4 -> 5; matrix products, arithmetic and copies ran while one was open for 8% -> 9% of each run, Pallas kernels for 0% -> 0%
where the time goes in v5:
time: 501 us; the launch traced here: 500 us
  waiting for transfers between devices  395 us (79%)
  starting transfers between devices  30.1 us (6%)
  other arithmetic  24.9 us (5%)
  matrix products  20.7 us (4%)
  local copies, waits for them, and re-layouts  15.4 us (3%)
  between operations  14.1 us (3%)
    all_to_all x2, waiting for transfers between devices, local(): lax.all_to_all(gradient.reshape(my_sample.shape), 'grp', split_axis=0, co...  181 us
    all_gather x1, waiting for transfers between devices, local(): group_x = lax.all_gather(tokens, 'shard', axis=0, tiled=True)  110 us
    all_to_all x2, waiting for transfers between devices, local(): lax.all_to_all(samples, 'grp', split_axis=0, concat_axis=0, tiled=True)  103 us
    dot_general x2, matrix products, contract_rows(): lax.dot_general(left, right, (((0,), (0,)), ((), ())), preferred_element_...  20.7 us
    all_to_all x2, starting transfers between devices, local(): lax.all_to_all(samples, 'grp', split_axis=0, concat_axis=0, tiled=True)  16.8 us
    convert_element_type x2, local copies, waits for them, and re-layouts, local(): gradient = contract_rows(group_x, residual).astype(jnp.bfloat16)  14.4 us
    all_to_all x2, starting transfers between devices, local(): lax.all_to_all(gradient.reshape(my_sample.shape), 'grp', split_axis=0, co...  13.3 us
    convert_element_type x2, other arithmetic, local(): (post_mean[None, :, lo:hi] + post_std[None, :, lo:hi] * noise_vals).astyp...  11.2 us
  transfers between devices with their start and end apart: 5, of which 5 were waited for; matrix products, arithmetic and copies ran while one was open for 9% of the time, Pallas kernels for 0%

profile of v5, /device:TPU:1, one launch (start us, length us, event | category | flops | bytes accessed | tf_op | source)
XLA Modules:
  0.0 500.3 jit_solution(14885875915672693368)
XLA Ops:
  7.2 1.0 slice.41
  8.1 1.1 multiply_rsqrt_fusion
  9.3 5.5 %fusion.4 = bf16[32,80,832]{2,1,0:T(8,128)(2,1)} fusion(f32[80,832]{1,0:T(8,128)S(1)} %slice.47, f32[80,832]{1,0:T(8,128)S(1)} %slice.41, bf16[32,80,1728]{2,1,0:T(8,128)(2,1)} %param.9), kind=kLoop, calls=%fused_computation.10 | loop fusion | flops 8519680 | bytes 9052160 | tf_op jit(solution)/shard_map/convert_element_type | solution.py:31
  14.9 0.0 slice-start
  14.9 10.2 %all-to-all-start.2 = ((bf16[32,80,832]{2,1,0:T(8,128)(2,1)}), bf16[32,80,832]{2,1,0:T(8,128)(2,1)}, u32[]{:S(2)}, u32[]{:S(2)}) async-start(bf16[32,80,832]{2,1,0:T(8,128)(2,1)} %fusion.4), calls=%async_computation.2 | async-start | bytes 9175040 | tf_op jit(solution)/shard_map/all_to_all | solution.py:34
  25.1 0.0 slice-done
  25.1 5.7 %fusion.1 = bf16[32,80,896]{2,1,0:T(8,128)(2,1)} fusion(f32[80,896]{1,0:T(8,128)S(1)} %slice.46, f32[80,896]{1,0:T(8,128)S(1)} %slice-done, bf16[32,80,1728]{2,1,0:T(8,128)(2,1)} %param.9), kind=kLoop, calls=%fused_computation.7 | loop fusion | flops 9175040 | bytes 9748480 | tf_op jit(solution)/shard_map/convert_element_type | solution.py:31
  30.8 95.9 %all-to-all-done.2 = bf16[32,80,832]{2,1,0:T(8,128)(2,1)} async-done(((bf16[32,80,832]{2,1,0:T(8,128)(2,1)}), bf16[32,80,832]{2,1,0:T(8,128)(2,1)}, u32[]{:S(2)}, u32[]{:S(2)}) %all-to-all-start.2) | async-done | bytes 4259872 | tf_op jit(solution)/shard_map/all_to_all | solution.py:34
  126.7 6.6 %all-to-all-start = ((bf16[32,80,896]{2,1,0:T(8,128)(2,1)}), bf16[32,80,896]{2,1,0:T(8,128)(2,1)}, u32[]{:S(2)}, u32[]{:S(2)}) async-start(bf16[32,80,896]{2,1,0:T(8,128)(2,1)} %fusion.1), calls=%async_computation | async-start | bytes 9175040 | tf_op jit(solution)/shard_map/all_to_all | solution.py:34
  133.3 0.0 all-gather.2.cloned.1.call-start
  133.4 0.7 all-gather.2.cloned.1.call-update
  134.1 110.5 %all-gather.2.cloned.1.call-done = bf16[512,2560]{1,0:T(8,128)(2,1)} async-done(((bf16[64,2560]{1,0:T(8,128)(2,1)}), bf16[512,2560]{1,0:T(8,128)(2,1)}) %all-gather.2.cloned.1.call-update) | async-done | bytes 2621456 | tf_op jit(solution)/shard_map/all_gather | solution.py:26
  244.5 11.1 %fusion.7 = bf16[2560,832]{0,1:T(8,128)(2,1)} fusion(bf16[512,2560]{1,0:T(8,128)(2,1)} %all-gather.2.cloned.1.call-done, bf16[2560,832]{1,0:T(8,128)(2,1)} %bitcast.4, bf16[512,1728]{0,1:T(8,128)(2,1)} %param.6), kind=kOutput, calls=%fused_computation.15 | convolution fusion | flops 4365484032 | bytes 14942208 | tf_op jit(solution)/shard_map/dot_general | solution.py:13
  255.6 7.1 %copy.10 = bf16[2560,832]{1,0:T(8,128)(2,1)} copy(bf16[2560,832]{0,1:T(8,128)(2,1)} %fusion.7) | data formatting | bytes 8519680 | tf_op jit(solution)/shard_map/convert_element_type | solution.py:43
  262.8 7.3 %all-to-all-done = bf16[32,80,896]{2,1,0:T(8,128)(2,1)} async-done(((bf16[32,80,896]{2,1,0:T(8,128)(2,1)}), bf16[32,80,896]{2,1,0:T(8,128)(2,1)}, u32[]{:S(2)}, u32[]{:S(2)}) %all-to-all-start) | async-done | bytes 4587552 | tf_op jit(solution)/shard_map/all_to_all | solution.py:34
  270.1 0.0 copy-start.2
  270.1 6.6 %all-to-all-start.3 = ((bf16[32,80,832]{2,1,0:T(8,128)(2,1)}), bf16[32,80,832]{2,1,0:T(8,128)(2,1)}, u32[]{:S(2)}, u32[]{:S(2)}) async-start(bf16[32,80,832]{2,1,0:T(8,128)(2,1)} %bitcast.27), calls=%async_computation.3 | async-start | bytes 9175040 | tf_op jit(solution)/shard_map/all_to_all | solution.py:44
  276.8 0.0 copy-done.2
  276.8 9.6 %fusion.6 = bf16[2560,896]{0,1:T(8,128)(2,1)} fusion(bf16[512,2560]{1,0:T(8,128)(2,1)S(1)} %copy-done.2, bf16[2560,896]{1,0:T(8,128)(2,1)} %bitcast, bf16[512,1728]{0,1:T(8,128)(2,1)} %param.6), kind=kOutput, calls=%fused_computation.14 | convolution fusion | flops 4701290496 | bytes 15335424 | tf_op jit(solution)/shard_map/dot_general | solution.py:13
  286.4 7.2 %copy.9 = bf16[2560,896]{1,0:T(8,128)(2,1)} copy(bf16[2560,896]{0,1:T(8,128)(2,1)} %fusion.6) | data formatting | bytes 9175040 | tf_op jit(solution)/shard_map/convert_element_type | solution.py:43
  293.6 84.8 %all-to-all-done.3 = bf16[32,80,832]{2,1,0:T(8,128)(2,1)} async-done(((bf16[32,80,832]{2,1,0:T(8,128)(2,1)}), bf16[32,80,832]{2,1,0:T(8,128)(2,1)}, u32[]{:S(2)}, u32[]{:S(2)}) %all-to-all-start.3) | async-done | bytes 4259872 | tf_op jit(solution)/shard_map/all_to_all | solution.py:44
  378.4 6.6 %all-to-all-start.1 = ((bf16[32,80,896]{2,1,0:T(8,128)(2,1)}), bf16[32,80,896]{2,1,0:T(8,128)(2,1)}, u32[]{:S(2)}, u32[]{:S(2)}) async-start(bf16[32,80,896]{2,1,0:T(8,128)(2,1)} %bitcast.26), calls=%async_computation.1 | async-start | bytes 9175040 | tf_op jit(solution)/shard_map/all_to_all | solution.py:44
  385.0 0.0 copy-start
  385.0 0.0 copy-start.1
  385.0 5.5 %convert_reduce_fusion = (f32[80,832]{1,0:T(8,128)S(1)}, f32[80,832]{1,0:T(8,128)S(1)}) fusion(bf16[32,80,832]{2,1,0:T(8,128)(2,1)} %all-to-all-done.3, bf16[32,80,1728]{2,1,0:T(8,128)(2,1)} %param.9), kind=kLoop, calls=%fused_computation.1 | loop fusion | flops 10516480 | bytes 9052160 | tf_op jit(solution)/shard_map/reduce_sum | solution.py:49
  390.5 0.0 copy-done
  390.6 0.0 copy-done.1
  390.6 0.2 divide_subtract_fusion
  390.8 95.9 %all-to-all-done.1 = bf16[32,80,896]{2,1,0:T(8,128)(2,1)} async-done(((bf16[32,80,896]{2,1,0:T(8,128)(2,1)}), bf16[32,80,896]{2,1,0:T(8,128)(2,1)}, u32[]{:S(2)}, u32[]{:S(2)}) %all-to-all-start.1) | async-done | bytes 4587552 | tf_op jit(solution)/shard_map/all_to_all | solution.py:44
  486.7 5.5 %convert_reduce_fusion.1 = (f32[80,896]{1,0:T(8,128)S(1)}, f32[80,896]{1,0:T(8,128)S(1)}) fusion(bf16[32,80,896]{2,1,0:T(8,128)(2,1)} %all-to-all-done.1, bf16[32,80,1728]{2,1,0:T(8,128)(2,1)} %param.9), kind=kLoop, calls=%fused_computation.4 | loop fusion | flops 11325440 | bytes 9748480 | tf_op jit(solution)/shard_map/reduce_sum | solution.py:49
  492.1 0.2 divide_subtract_fusion.1
  492.3 1.1 pad_maximum_fusion
  (2 shorter events, 0.0 us)
Async XLA Ops:
  14.9 10.2 %slice-start = ((f32[80,1728]{1,0:T(8,128)}), f32[80,896]{1,0:T(8,128)S(1)}, s32[]{:S(2)}) async-start(f32[80,1728]{1,0:T(8,128)} %param.7), calls=%async_computation.5 | async-start | bytes 573440 | tf_op jit(solution)/shard_map/slice | solution.py:47
  14.9 111.8 %all-to-all-start.2 = ((bf16[32,80,832]{2,1,0:T(8,128)(2,1)}), bf16[32,80,832]{2,1,0:T(8,128)(2,1)}, u32[]{:S(2)}, u32[]{:S(2)}) async-start(bf16[32,80,832]{2,1,0:T(8,128)(2,1)} %fusion.4), calls=%async_computation.2 | async-start | bytes 9175040 | tf_op jit(solution)/shard_map/all_to_all | solution.py:34
  126.7 143.4 %all-to-all-start = ((bf16[32,80,896]{2,1,0:T(8,128)(2,1)}), bf16[32,80,896]{2,1,0:T(8,128)(2,1)}, u32[]{:S(2)}, u32[]{:S(2)}) async-start(bf16[32,80,896]{2,1,0:T(8,128)(2,1)} %fusion.1), calls=%async_computation | async-start | bytes 9175040 | tf_op jit(solution)/shard_map/all_to_all | solution.py:34
  133.3 111.2 %all-gather.2.cloned.1.call-start = ((), (), s32[]{:S(2)}) async-start(), calls=%async_computation.4 | async-start | bytes 2949120 | tf_op jit(solution)/shard_map/all_gather | solution.py:26
  270.1 6.7 %copy-start.2 = (bf16[512,2560]{1,0:T(8,128)(2,1)S(1)}, bf16[512,2560]{1,0:T(8,128)(2,1)}, u32[]{:S(2)}) copy-start(bf16[512,2560]{1,0:T(8,128)(2,1)} %all-gather.2.cloned.1.call-done) | copy-start | bytes 7864324
  270.1 108.3 %all-to-all-start.3 = ((bf16[32,80,832]{2,1,0:T(8,128)(2,1)}), bf16[32,80,832]{2,1,0:T(8,128)(2,1)}, u32[]{:S(2)}, u32[]{:S(2)}) async-start(bf16[32,80,832]{2,1,0:T(8,128)(2,1)} %bitcast.27), calls=%async_computation.3 | async-start | bytes 9175040 | tf_op jit(solution)/shard_map/all_to_all | solution.py:44
  378.4 108.3 %all-to-all-start.1 = ((bf16[32,80,896]{2,1,0:T(8,128)(2,1)}), bf16[32,80,896]{2,1,0:T(8,128)(2,1)}, u32[]{:S(2)}, u32[]{:S(2)}) async-start(bf16[32,80,896]{2,1,0:T(8,128)(2,1)} %bitcast.26), calls=%async_computation.1 | async-start | bytes 9175040 | tf_op jit(solution)/shard_map/all_to_all | solution.py:44
  385.0 5.5 %copy-start = (f32[80,1728]{1,0:T(8,128)S(1)}, f32[80,1728]{1,0:T(8,128)}, u32[]{:S(2)}) copy-start(f32[80,1728]{1,0:T(8,128)} %param.8) | copy-start | bytes 1658884
  385.0 5.5 %copy-start.1 = (f32[80,1728]{1,0:T(8,128)S(1)}, f32[80,1728]{1,0:T(8,128)}, u32[]{:S(2)}) copy-start(f32[80,1728]{1,0:T(8,128)} %param.7) | copy-start | bytes 1658884
Sparse Core Ops, SparseCore 0:
  136.7 107.7 all-gather.1

commit v6 on v5

--- a/solution.py
+++ b/solution.py
@@ -23,7 +23,16 @@
 def local(tokens, target, post_mean, post_hess, weight_noise):
     groups = weight_noise.shape[0]
     post_std = lax.rsqrt(sample_size * (post_hess + weight_decay))
-    group_x = lax.all_gather(tokens, "shard", axis=0, tiled=True)
+    n_shard = lax.axis_size("shard")
+    me_s = lax.axis_index("shard")
+    blocks = [tokens] + [
+        lax.ppermute(tokens, "shard", [(i, (i - d) % n_shard) for i in range(n_shard)])
+        for d in range(1, n_shard)
+    ]
+    doubled = jnp.concatenate(blocks + blocks, axis=0)
+    group_x = lax.dynamic_slice_in_dim(
+        doubled, ((n_shard - me_s) % n_shard) * tokens.shape[0], n_shard * tokens.shape[0], axis=0
+    )
     chunks = column_chunks(weight_noise.shape[-1])
     my_samples = []
     for lo, hi in chunks:

time: 501 us -> 531 us (1.060)
  waiting for transfers between devices: 395 us -> 422 us
  starting transfers between devices: 30.1 us -> 49.8 us
  between operations: 14.1 us -> 0.88 us
    ppermute x0 -> x7, waiting for transfers between devices: none -> 140 us  [local(): lax.ppermute(tokens, 'shard', [(i, (i - d) % n_shard) for i in range(n_sh...]
    all_gather x1 -> x0, waiting for transfers between devices: 110 us -> none  [local(): group_x = lax.all_gather(tokens, 'shard', axis=0, tiled=True)]
    ppermute x0 -> x7, starting transfers between devices: none -> 12.9 us  [local(): lax.ppermute(tokens, 'shard', [(i, (i - d) % n_shard) for i in range(n_sh...]
    all_to_all x2, waiting for transfers between devices: 103 us -> 95.9 us  [local(): lax.all_to_all(samples, 'grp', split_axis=0, concat_axis=0, tiled=True)]
    convert_element_type x2 -> x1, local copies, waits for them, and re-layouts: 14.4 us -> 7.12 us  [local(): gradient = contract_rows(group_x, residual).astype(jnp.bfloat16)]
    all_to_all x2, starting transfers between devices: 13.3 us -> 20.1 us  [local(): lax.all_to_all(gradient.reshape(my_sample.shape), 'grp', split_axis=0, co...]
    all_to_all x2, waiting for transfers between devices: 181 us -> 186 us  [local(): lax.all_to_all(gradient.reshape(my_sample.shape), 'grp', split_axis=0, co...]
  transfers between devices with their start and end apart: 5 -> 11, of which waited for: 5 -> 8; matrix products, arithmetic and copies ran while one was open for 9% -> 8% of each run, Pallas kernels for 0% -> 0%
where the time goes in v6:
time: 531 us; the launch traced here: 530 us
  waiting for transfers between devices  422 us (79%)
  starting transfers between devices  49.8 us (9%)
  other arithmetic  24.8 us (5%)
  matrix products  22.2 us (4%)
  local copies, waits for them, and re-layouts  10.8 us (2%)
    all_to_all x2, waiting for transfers between devices, local(): lax.all_to_all(gradient.reshape(my_sample.shape), 'grp', split_axis=0, co...  186 us
    ppermute x7, waiting for transfers between devices, local(): lax.ppermute(tokens, 'shard', [(i, (i - d) % n_shard) for i in range(n_sh...  140 us
    all_to_all x2, waiting for transfers between devices, local(): lax.all_to_all(samples, 'grp', split_axis=0, concat_axis=0, tiled=True)  95.9 us
    dot_general x2, matrix products, contract_rows(): lax.dot_general(left, right, (((0,), (0,)), ((), ())), preferred_element_...  22.2 us
    all_to_all x2, starting transfers between devices, local(): lax.all_to_all(gradient.reshape(my_sample.shape), 'grp', split_axis=0, co...  20.1 us
    all_to_all x2, starting transfers between devices, local(): lax.all_to_all(samples, 'grp', split_axis=0, concat_axis=0, tiled=True)  16.8 us
    ppermute x7, starting transfers between devices, local(): lax.ppermute(tokens, 'shard', [(i, (i - d) % n_shard) for i in range(n_sh...  12.9 us
    convert_element_type x2, other arithmetic, local(): (post_mean[None, :, lo:hi] + post_std[None, :, lo:hi] * noise_vals).astyp...  11.2 us
  transfers between devices with their start and end apart: 11, of which 8 were waited for; matrix products, arithmetic and copies ran while one was open for 8% of the time, Pallas kernels for 0%

profile of v6, /device:TPU:1, one launch (start us, length us, event | category | flops | bytes accessed | tf_op | source)
XLA Modules:
  0.0 530.0 jit_solution(10888909712989873139)
XLA Ops:
  0.6 1.1 multiply_rsqrt_fusion
  1.8 1.0 slice.41
  2.8 5.5 %fusion.4 = bf16[32,80,832]{2,1,0:T(8,128)(2,1)} fusion(f32[80,832]{1,0:T(8,128)S(1)} %slice.47, f32[80,832]{1,0:T(8,128)S(1)} %slice.41, bf16[32,80,1728]{2,1,0:T(8,128)(2,1)} %param.9), kind=kLoop, calls=%fused_computation.10 | loop fusion | flops 8519680 | bytes 9052160 | tf_op jit(solution)/shard_map/convert_element_type | solution.py:40
  8.3 10.2 %all-to-all-start.2 = ((bf16[32,80,832]{2,1,0:T(8,128)(2,1)}), bf16[32,80,832]{2,1,0:T(8,128)(2,1)}, u32[]{:S(2)}, u32[]{:S(2)}) async-start(bf16[32,80,832]{2,1,0:T(8,128)(2,1)} %fusion.4), calls=%async_computation.2 | async-start | bytes 9175040 | tf_op jit(solution)/shard_map/all_to_all | solution.py:43
  18.6 5.7 %fusion.1 = bf16[32,80,896]{2,1,0:T(8,128)(2,1)} fusion(f32[80,896]{1,0:T(8,128)S(1)} %slice.46, f32[80,896]{1,0:T(8,128)S(1)} %slice-done, bf16[32,80,1728]{2,1,0:T(8,128)(2,1)} %param.9), kind=kLoop, calls=%fused_computation.7 | loop fusion | flops 9175040 | bytes 9748480 | tf_op jit(solution)/shard_map/convert_element_type | solution.py:40
  24.2 95.9 %all-to-all-done.2 = bf16[32,80,832]{2,1,0:T(8,128)(2,1)} async-done(((bf16[32,80,832]{2,1,0:T(8,128)(2,1)}), bf16[32,80,832]{2,1,0:T(8,128)(2,1)}, u32[]{:S(2)}, u32[]{:S(2)}) %all-to-all-start.2) | async-done | bytes 4259872 | tf_op jit(solution)/shard_map/all_to_all | solution.py:43
  120.2 6.6 %all-to-all-start = ((bf16[32,80,896]{2,1,0:T(8,128)(2,1)}), bf16[32,80,896]{2,1,0:T(8,128)(2,1)}, u32[]{:S(2)}, u32[]{:S(2)}) async-start(bf16[32,80,896]{2,1,0:T(8,128)(2,1)} %fusion.1), calls=%async_computation | async-start | bytes 9175040 | tf_op jit(solution)/shard_map/all_to_all | solution.py:43
  126.8 6.7 %collective-permute-start = (bf16[64,2560]{1,0:T(8,128)(2,1)S(1)}, bf16[64,2560]{1,0:T(8,128)(2,1)S(1)}, u32[]{:S(2)}, u32[]{:S(2)}) collective-permute-start(bf16[64,2560]{1,0:T(8,128)(2,1)S(1)} %copy-done.2), channel_id=1, source_target_pairs={{0,7},{1,0},{2,1},{3,2},{4,3},{5,4},{6,5},{7,6},{8,15},{9,8},{10,9... | collective-permute-start | bytes 983048 | tf_op jit(solution)/shard_map/ppermute | solution.py:29
  133.5 0.3 collective-permute-start.1
  133.9 1.6 collective-permute-start.2
  135.5 4.2 collective-permute-start.3
  139.7 110.0 %collective-permute-done = bf16[64,2560]{1,0:T(8,128)(2,1)S(1)} collective-permute-done((bf16[64,2560]{1,0:T(8,128)(2,1)S(1)}, bf16[64,2560]{1,0:T(8,128)(2,1)S(1)}, u32[]{:S(2)}, u32[]{:S(2)}) %collective-permute-start) | collective-permute-done | bytes 327712 | tf_op jit(solution)/shard_map/ppermute | solution.py:29
  249.8 9.3 %collective-permute-done.1 = bf16[64,2560]{1,0:T(8,128)(2,1)S(1)} collective-permute-done((bf16[64,2560]{1,0:T(8,128)(2,1)S(1)}, bf16[64,2560]{1,0:T(8,128)(2,1)S(1)}, u32[]{:S(2)}, u32[]{:S(2)}) %collective-permute-start.1) | collective-permute-done | bytes 327712 | tf_op jit(solution)/shard_map/ppermute | solution.py:29
  259.1 0.0 collective-permute-start.6
  259.1 11.9 %collective-permute-done.2 = bf16[64,2560]{1,0:T(8,128)(2,1)S(1)} collective-permute-done((bf16[64,2560]{1,0:T(8,128)(2,1)S(1)}, bf16[64,2560]{1,0:T(8,128)(2,1)S(1)}, u32[]{:S(2)}, u32[]{:S(2)}) %collective-permute-start.2) | collective-permute-done | bytes 327712 | tf_op jit(solution)/shard_map/ppermute | solution.py:29
  271.0 7.0 %collective-permute-done.3 = bf16[64,2560]{1,0:T(8,128)(2,1)S(1)} collective-permute-done((bf16[64,2560]{1,0:T(8,128)(2,1)S(1)}, bf16[64,2560]{1,0:T(8,128)(2,1)S(1)}, u32[]{:S(2)}, u32[]{:S(2)}) %collective-permute-start.3) | collective-permute-done | bytes 327712 | tf_op jit(solution)/shard_map/ppermute | solution.py:29
  278.1 1.3 collective-permute-done.6
  279.7 2.3 copy-done.3
  282.1 10.8 %convolution_convert_fusion.1 = bf16[2560,832]{0,1:T(8,128)(2,1)} fusion(bf16[1024,2560]{1,0:T(8,128)(2,1)} %copy-done.3, s32[]{:T(128)S(6)} %select_n.11, bf16[2560,832]{1,0:T(8,128)(2,1)} %bitcast.2, bf16[512,1728]{0,1:T(8,128)(2,1)} %param.6), kind=kOutput, calls=%fused_computation.13 | convolution fusion | flops 4365484032 | bytes 14943232 | tf_op jit(solution)/shard_map/dot_general | solution.py:13
  292.8 7.1 %copy.8 = bf16[2560,832]{1,0:T(8,128)(2,1)} copy(bf16[2560,832]{0,1:T(8,128)(2,1)} %convolution_convert_fusion.1) | data formatting | bytes 8519680 | tf_op jit(solution)/shard_map/convert_element_type | solution.py:52
  300.0 13.5 %all-to-all-start.3 = ((bf16[32,80,832]{2,1,0:T(8,128)(2,1)}), bf16[32,80,832]{2,1,0:T(8,128)(2,1)}, u32[]{:S(2)}, u32[]{:S(2)}) async-start(bf16[32,80,832]{2,1,0:T(8,128)(2,1)} %bitcast.11), calls=%async_computation.3 | async-start | bytes 9175040 | tf_op jit(solution)/shard_map/all_to_all | solution.py:53
  313.5 11.4 %convolution_convert_fusion = bf16[2560,896]{1,0:T(8,128)(2,1)} fusion(bf16[1024,2560]{1,0:T(8,128)(2,1)} %copy-done.3, s32[]{:T(128)S(6)} %select_n.11, bf16[2560,896]{1,0:T(8,128)(2,1)} %bitcast, bf16[512,1728]{0,1:T(8,128)(2,1)S(1)} %copy-done.4), kind=kOutput, calls=%fused_computation.12 | convolution fusion | flops 4701290496 | bytes 15336448 | tf_op jit(solution)/shard_map/dot_general | solution.py:13
  324.8 90.2 %all-to-all-done.3 = bf16[32,80,832]{2,1,0:T(8,128)(2,1)} async-done(((bf16[32,80,832]{2,1,0:T(8,128)(2,1)}), bf16[32,80,832]{2,1,0:T(8,128)(2,1)}, u32[]{:S(2)}, u32[]{:S(2)}) %all-to-all-start.3) | async-done | bytes 4259872 | tf_op jit(solution)/shard_map/all_to_all | solution.py:53
  415.1 6.6 %all-to-all-start.1 = ((bf16[32,80,896]{2,1,0:T(8,128)(2,1)}), bf16[32,80,896]{2,1,0:T(8,128)(2,1)}, u32[]{:S(2)}, u32[]{:S(2)}) async-start(bf16[32,80,896]{2,1,0:T(8,128)(2,1)} %bitcast.12), calls=%async_computation.1 | async-start | bytes 9175040 | tf_op jit(solution)/shard_map/all_to_all | solution.py:53
  421.7 0.0 copy-start
  421.7 0.0 copy-start.1
  421.7 5.5 %convert_reduce_fusion = (f32[80,832]{1,0:T(8,128)S(1)}, f32[80,832]{1,0:T(8,128)S(1)}) fusion(bf16[32,80,832]{2,1,0:T(8,128)(2,1)} %all-to-all-done.3, bf16[32,80,1728]{2,1,0:T(8,128)(2,1)} %param.9), kind=kLoop, calls=%fused_computation.1 | loop fusion | flops 10516480 | bytes 9052160 | tf_op jit(solution)/shard_map/reduce_sum | solution.py:58
  427.3 0.2 divide_subtract_fusion
  427.5 95.9 %all-to-all-done.1 = bf16[32,80,896]{2,1,0:T(8,128)(2,1)} async-done(((bf16[32,80,896]{2,1,0:T(8,128)(2,1)}), bf16[32,80,896]{2,1,0:T(8,128)(2,1)}, u32[]{:S(2)}, u32[]{:S(2)}) %all-to-all-start.1) | async-done | bytes 4587552 | tf_op jit(solution)/shard_map/all_to_all | solution.py:53
  523.4 5.4 %convert_reduce_fusion.1 = (f32[80,896]{1,0:T(8,128)S(1)}, f32[80,896]{1,0:T(8,128)S(1)}) fusion(bf16[32,80,896]{2,1,0:T(8,128)(2,1)} %all-to-all-done.1, bf16[32,80,1728]{2,1,0:T(8,128)(2,1)} %param.9), kind=kLoop, calls=%fused_computation.4 | loop fusion | flops 11325440 | bytes 9748480 | tf_op jit(solution)/shard_map/reduce_sum | solution.py:58
  528.7 0.2 divide_subtract_fusion.1
  529.0 1.1 pad_maximum_fusion
  (32 shorter events, 0.4 us)
Async XLA Ops:
  8.3 10.2 %slice-start = ((f32[80,1728]{1,0:T(8,128)}), f32[80,896]{1,0:T(8,128)S(1)}, s32[]{:S(2)}) async-start(f32[80,1728]{1,0:T(8,128)} %param.7), calls=%async_computation.4 | async-start | bytes 573440 | tf_op jit(solution)/shard_map/slice | solution.py:56
  8.3 111.8 %all-to-all-start.2 = ((bf16[32,80,832]{2,1,0:T(8,128)(2,1)}), bf16[32,80,832]{2,1,0:T(8,128)(2,1)}, u32[]{:S(2)}, u32[]{:S(2)}) async-start(bf16[32,80,832]{2,1,0:T(8,128)(2,1)} %fusion.4), calls=%async_computation.2 | async-start | bytes 9175040 | tf_op jit(solution)/shard_map/all_to_all | solution.py:43
  24.2 102.5 %copy-start.2 = (bf16[64,2560]{1,0:T(8,128)(2,1)S(1)}, bf16[64,2560]{1,0:T(8,128)(2,1)}, u32[]{:S(2)}) copy-start(bf16[64,2560]{1,0:T(8,128)(2,1)} %param.5) | copy-start | bytes 983044
  120.2 179.8 %all-to-all-start = ((bf16[32,80,896]{2,1,0:T(8,128)(2,1)}), bf16[32,80,896]{2,1,0:T(8,128)(2,1)}, u32[]{:S(2)}, u32[]{:S(2)}) async-start(bf16[32,80,896]{2,1,0:T(8,128)(2,1)} %fusion.1), calls=%async_computation | async-start | bytes 9175040 | tf_op jit(solution)/shard_map/all_to_all | solution.py:43
  126.8 122.9 %collective-permute-start = (bf16[64,2560]{1,0:T(8,128)(2,1)S(1)}, bf16[64,2560]{1,0:T(8,128)(2,1)S(1)}, u32[]{:S(2)}, u32[]{:S(2)}) collective-permute-start(bf16[64,2560]{1,0:T(8,128)(2,1)S(1)} %copy-done.2), channel_id=1, source_target_pairs={{0,7},{1,0},{2,1},{3,2},{4,3},{5,4},{6,5},{7,6},{8,15},{9,8},{10,9... | collective-permute-start | bytes 983048 | tf_op jit(solution)/shard_map/ppermute | solution.py:29
  133.5 125.6 %collective-permute-start.1 = (bf16[64,2560]{1,0:T(8,128)(2,1)S(1)}, bf16[64,2560]{1,0:T(8,128)(2,1)S(1)}, u32[]{:S(2)}, u32[]{:S(2)}) collective-permute-start(bf16[64,2560]{1,0:T(8,128)(2,1)S(1)} %copy-done.2), channel_id=1, source_target_pairs={{0,6},{1,7},{2,0},{3,1},{4,2},{5,3},{6,4},{7,5},{8,14},{9,15},{10,... | collective-permute-start | bytes 983048 | tf_op jit(solution)/shard_map/ppermute | solution.py:29
  133.9 137.1 %collective-permute-start.2 = (bf16[64,2560]{1,0:T(8,128)(2,1)S(1)}, bf16[64,2560]{1,0:T(8,128)(2,1)S(1)}, u32[]{:S(2)}, u32[]{:S(2)}) collective-permute-start(bf16[64,2560]{1,0:T(8,128)(2,1)S(1)} %copy-done.2), channel_id=1, source_target_pairs={{0,5},{1,6},{2,7},{3,0},{4,1},{5,2},{6,3},{7,4},{8,13},{9,14},{10,... | collective-permute-start | bytes 983048 | tf_op jit(solution)/shard_map/ppermute | solution.py:29
  135.5 142.6 %collective-permute-start.3 = (bf16[64,2560]{1,0:T(8,128)(2,1)S(1)}, bf16[64,2560]{1,0:T(8,128)(2,1)S(1)}, u32[]{:S(2)}, u32[]{:S(2)}) collective-permute-start(bf16[64,2560]{1,0:T(8,128)(2,1)S(1)} %copy-done.2), channel_id=1, source_target_pairs={{0,4},{1,5},{2,6},{3,7},{4,0},{5,1},{6,2},{7,3},{8,12},{9,13},{10,... | collective-permute-start | bytes 983048 | tf_op jit(solution)/shard_map/ppermute | solution.py:29
  139.7 138.4 %collective-permute-start.4 = (bf16[64,2560]{1,0:T(8,128)(2,1)S(1)}, bf16[64,2560]{1,0:T(8,128)(2,1)S(1)}, u32[]{:S(2)}, u32[]{:S(2)}) collective-permute-start(bf16[64,2560]{1,0:T(8,128)(2,1)S(1)} %copy-done.2), channel_id=1, source_target_pairs={{0,3},{1,4},{2,5},{3,6},{4,7},{5,0},{6,1},{7,2},{8,11},{9,12},{10,... | collective-permute-start | bytes 983048 | tf_op jit(solution)/shard_map/ppermute | solution.py:29
  249.7 28.3 %collective-permute-start.5 = (bf16[64,2560]{1,0:T(8,128)(2,1)S(1)}, bf16[64,2560]{1,0:T(8,128)(2,1)S(1)}, u32[]{:S(2)}, u32[]{:S(2)}) collective-permute-start(bf16[64,2560]{1,0:T(8,128)(2,1)S(1)} %copy-done.2), channel_id=1, source_target_pairs={{0,2},{1,3},{2,4},{3,5},{4,6},{5,7},{6,0},{7,1},{8,10},{9,11},{10,... | collective-permute-start | bytes 983048 | tf_op jit(solution)/shard_map/ppermute | solution.py:29
  259.1 20.4 %collective-permute-start.6 = (bf16[64,2560]{1,0:T(8,128)(2,1)S(1)}, bf16[64,2560]{1,0:T(8,128)(2,1)S(1)}, u32[]{:S(2)}, u32[]{:S(2)}) collective-permute-start(bf16[64,2560]{1,0:T(8,128)(2,1)S(1)} %copy-done.2), channel_id=1, source_target_pairs={{0,1},{1,2},{2,3},{3,4},{4,5},{5,6},{6,7},{7,0},{8,9},{9,10},{10,1... | collective-permute-start | bytes 983048 | tf_op jit(solution)/shard_map/ppermute | solution.py:29
  279.7 2.3 copy-start.3
  300.0 13.5 %copy-start.4 = (bf16[512,1728]{0,1:T(8,128)(2,1)S(1)}, bf16[512,1728]{0,1:T(8,128)(2,1)}, u32[]{:S(2)}) copy-start(bf16[512,1728]{0,1:T(8,128)(2,1)} %param.6) | copy-start | bytes 5308420
  300.0 115.1 %all-to-all-start.3 = ((bf16[32,80,832]{2,1,0:T(8,128)(2,1)}), bf16[32,80,832]{2,1,0:T(8,128)(2,1)}, u32[]{:S(2)}, u32[]{:S(2)}) async-start(bf16[32,80,832]{2,1,0:T(8,128)(2,1)} %bitcast.11), calls=%async_computation.3 | async-start | bytes 9175040 | tf_op jit(solution)/shard_map/all_to_all | solution.py:53
  415.1 108.3 %all-to-all-start.1 = ((bf16[32,80,896]{2,1,0:T(8,128)(2,1)}), bf16[32,80,896]{2,1,0:T(8,128)(2,1)}, u32[]{:S(2)}, u32[]{:S(2)}) async-start(bf16[32,80,896]{2,1,0:T(8,128)(2,1)} %bitcast.12), calls=%async_computation.1 | async-start | bytes 9175040 | tf_op jit(solution)/shard_map/all_to_all | solution.py:53
  421.7 5.5 %copy-start = (f32[80,1728]{1,0:T(8,128)S(1)}, f32[80,1728]{1,0:T(8,128)}, u32[]{:S(2)}) copy-start(f32[80,1728]{1,0:T(8,128)} %param.8) | copy-start | bytes 1658884
  421.7 5.5 %copy-start.1 = (f32[80,1728]{1,0:T(8,128)S(1)}, f32[80,1728]{1,0:T(8,128)}, u32[]{:S(2)}) copy-start(f32[80,1728]{1,0:T(8,128)} %param.7) | copy-start | bytes 1658884

commit v7 on v5

--- a/solution.py
+++ b/solution.py
@@ -2,6 +2,7 @@
 import jax.numpy as jnp
 from jax import lax
 from jax.sharding import PartitionSpec as P
+
 
 sample_size = 50.0
 weight_decay = 0.02
@@ -23,7 +24,10 @@
 def local(tokens, target, post_mean, post_hess, weight_noise):
     groups = weight_noise.shape[0]
     post_std = lax.rsqrt(sample_size * (post_hess + weight_decay))
-    group_x = lax.all_gather(tokens, "shard", axis=0, tiled=True)
+    half = tokens.shape[1] // 2
+    x_a = lax.all_gather(tokens[:, :half], "shard", axis=0, tiled=True)
+    x_b = lax.all_gather(tokens[:, half:], "shard", axis=0, tiled=True)
+    group_x = jnp.concatenate([x_a, x_b], axis=1)
     chunks = column_chunks(weight_noise.shape[-1])
     my_samples = []
     for lo, hi in chunks:

time: 501 us -> 534 us (1.066)
  waiting for transfers between devices: 395 us -> 431 us
    all_gather x1 -> x2, waiting for transfers between devices: 110 us -> 147 us  [the longest x1 79.6 us: local(): x_a = lax.all_gather(tokens[:, :half], 'shard', axis=0, tiled=True)]
    all_to_all x2, waiting for transfers between devices: 103 us -> 96 us  [local(): lax.all_to_all(samples, 'grp', split_axis=0, concat_axis=0, tiled=True)]
    convert_element_type x2 -> x1, local copies, waits for them, and re-layouts: 14.4 us -> 7.13 us  [local(): gradient = contract_rows(group_x, residual).astype(jnp.bfloat16)]
    all_to_all x2, waiting for transfers between devices: 181 us -> 188 us  [local(): lax.all_to_all(gradient.reshape(my_sample.shape), 'grp', split_axis=0, co...]
  transfers between devices with their start and end apart: 5 -> 6, of which waited for: 5 -> 5; matrix products, arithmetic and copies ran while one was open for 9% -> 8% of each run, Pallas kernels for 0% -> 0%
where the time goes in v7:
time: 534 us; the launch traced here: 533 us
  waiting for transfers between devices  431 us (81%)
  starting transfers between devices  31.9 us (6%)
  other arithmetic  24.7 us (5%)
  matrix products  19.1 us (4%)
  between operations  14.2 us (3%)
  local copies, waits for them, and re-layouts  11.7 us (2%)
    all_to_all x2, waiting for transfers between devices, local(): lax.all_to_all(gradient.reshape(my_sample.shape), 'grp', split_axis=0, co...  188 us
    all_to_all x2, waiting for transfers between devices, local(): lax.all_to_all(samples, 'grp', split_axis=0, concat_axis=0, tiled=True)  96 us
    all_gather x1, waiting for transfers between devices, local(): x_a = lax.all_gather(tokens[:, :half], 'shard', axis=0, tiled=True)  79.6 us
    all_gather x1, waiting for transfers between devices, local(): x_b = lax.all_gather(tokens[:, half:], 'shard', axis=0, tiled=True)  67.6 us
    dot_general x2, matrix products, contract_rows(): lax.dot_general(left, right, (((0,), (0,)), ((), ())), preferred_element_...  19.1 us
    all_to_all x2, starting transfers between devices, local(): lax.all_to_all(samples, 'grp', split_axis=0, concat_axis=0, tiled=True)  16.8 us
    all_to_all x2, starting transfers between devices, local(): lax.all_to_all(gradient.reshape(my_sample.shape), 'grp', split_axis=0, co...  15.1 us
    convert_element_type x2, other arithmetic, local(): (post_mean[None, :, lo:hi] + post_std[None, :, lo:hi] * noise_vals).astyp...  11.1 us
  transfers between devices with their start and end apart: 6, of which 5 were waited for; matrix products, arithmetic and copies ran while one was open for 8% of the time, Pallas kernels for 0%

profile of v7, /device:TPU:1, one launch (start us, length us, event | category | flops | bytes accessed | tf_op | source)
XLA Modules:
  0.0 533.0 jit_solution(10131862466876454085)
XLA Ops:
  7.2 1.0 slice.49
  8.1 1.1 multiply_rsqrt_fusion
  9.3 5.5 %fusion.4 = bf16[32,80,832]{2,1,0:T(8,128)(2,1)} fusion(f32[80,832]{1,0:T(8,128)S(1)} %slice.55, f32[80,832]{1,0:T(8,128)S(1)} %slice.49, bf16[32,80,1728]{2,1,0:T(8,128)(2,1)} %param.9), kind=kLoop, calls=%fused_computation.10 | loop fusion | flops 8519680 | bytes 9052160 | tf_op jit(solution)/shard_map/convert_element_type | solution.py:35
  14.9 10.2 %all-to-all-start.2 = ((bf16[32,80,832]{2,1,0:T(8,128)(2,1)}), bf16[32,80,832]{2,1,0:T(8,128)(2,1)}, u32[]{:S(2)}, u32[]{:S(2)}) async-start(bf16[32,80,832]{2,1,0:T(8,128)(2,1)} %fusion.4), calls=%async_computation.2 | async-start | bytes 9175040 | tf_op jit(solution)/shard_map/all_to_all | solution.py:38
  25.1 5.6 %fusion.1 = bf16[32,80,896]{2,1,0:T(8,128)(2,1)} fusion(f32[80,896]{1,0:T(8,128)S(1)} %slice.54, f32[80,896]{1,0:T(8,128)S(1)} %slice-done, bf16[32,80,1728]{2,1,0:T(8,128)(2,1)} %param.9), kind=kLoop, calls=%fused_computation.7 | loop fusion | flops 9175040 | bytes 9748480 | tf_op jit(solution)/shard_map/convert_element_type | solution.py:35
  30.7 96.0 %all-to-all-done.2 = bf16[32,80,832]{2,1,0:T(8,128)(2,1)} async-done(((bf16[32,80,832]{2,1,0:T(8,128)(2,1)}), bf16[32,80,832]{2,1,0:T(8,128)(2,1)}, u32[]{:S(2)}, u32[]{:S(2)}) %all-to-all-start.2) | async-done | bytes 4259872 | tf_op jit(solution)/shard_map/all_to_all | solution.py:38
  126.7 6.6 %all-to-all-start = ((bf16[32,80,896]{2,1,0:T(8,128)(2,1)}), bf16[32,80,896]{2,1,0:T(8,128)(2,1)}, u32[]{:S(2)}, u32[]{:S(2)}) async-start(bf16[32,80,896]{2,1,0:T(8,128)(2,1)} %fusion.1), calls=%async_computation | async-start | bytes 9175040 | tf_op jit(solution)/shard_map/all_to_all | solution.py:38
  133.3 0.0 all-gather.3.cloned.1.call-start
  133.4 0.0 copy-done.2
  133.4 0.7 fusion.12
  134.1 0.0 all-gather.3.cloned.1.call-update
  134.1 0.0 all-gather.5.cloned.1.call-start
  134.2 0.7 all-gather.5.cloned.1.call-update
  134.9 79.6 %all-gather.3.cloned.1.call-done = bf16[512,1280]{1,0:T(8,128)(2,1)} async-done(((bf16[64,1280]{1,0:T(8,128)(2,1)}), bf16[512,1280]{1,0:T(8,128)(2,1)}) %all-gather.3.cloned.1.call-update) | async-done | bytes 1310736 | tf_op jit(solution)/shard_map/all_gather | solution.py:28
  214.5 1.4 constant_dynamic-update-slice_fusion.1
  215.9 67.6 %all-gather.5.cloned.1.call-done = bf16[512,1280]{1,0:T(8,128)(2,1)} async-done(((bf16[64,1280]{1,0:T(8,128)(2,1)}), bf16[512,1280]{1,0:T(8,128)(2,1)}) %all-gather.5.cloned.1.call-update) | async-done | bytes 1310736 | tf_op jit(solution)/shard_map/all_gather | solution.py:29
  283.5 1.4 constant_dynamic-update-slice_fusion
  284.9 9.1 %convolution_convert_fusion.1 = bf16[2560,832]{0,1:T(8,128)(2,1)} fusion(bf16[512,2560]{1,0:T(8,128)(2,1)S(1)} %constant_dynamic-update-slice_fusion, bf16[2560,832]{1,0:T(8,128)(2,1)} %bitcast.2, bf16[512,1728]{0,1:T(8,128)(2,1)} %param.6), kind=kOutput, calls=%fused_computation.13 | convolution fusion | flops 4365484032 | bytes 14942208 | tf_op jit(solution)/shard_map/dot_general | solution.py:14
  294.0 7.1 %copy.8 = bf16[2560,832]{1,0:T(8,128)(2,1)} copy(bf16[2560,832]{0,1:T(8,128)(2,1)} %convolution_convert_fusion.1) | data formatting | bytes 8519680 | tf_op jit(solution)/shard_map/convert_element_type | solution.py:47
  301.2 0.0 all-to-all-done
  301.2 8.4 %all-to-all-start.3 = ((bf16[32,80,832]{2,1,0:T(8,128)(2,1)}), bf16[32,80,832]{2,1,0:T(8,128)(2,1)}, u32[]{:S(2)}, u32[]{:S(2)}) async-start(bf16[32,80,832]{2,1,0:T(8,128)(2,1)} %bitcast.10), calls=%async_computation.3 | async-start | bytes 9175040 | tf_op jit(solution)/shard_map/all_to_all | solution.py:48
  309.6 10.0 %convolution_convert_fusion = bf16[2560,896]{1,0:T(8,128)(2,1)} fusion(bf16[512,2560]{1,0:T(8,128)(2,1)S(1)} %constant_dynamic-update-slice_fusion, bf16[2560,896]{1,0:T(8,128)(2,1)} %bitcast, bf16[512,1728]{0,1:T(8,128)(2,1)} %param.6), kind=kOutput, calls=%fused_computation.12 | convolution fusion | flops 4701290496 | bytes 15335424 | tf_op jit(solution)/shard_map/dot_general | solution.py:14
  319.6 91.7 %all-to-all-done.3 = bf16[32,80,832]{2,1,0:T(8,128)(2,1)} async-done(((bf16[32,80,832]{2,1,0:T(8,128)(2,1)}), bf16[32,80,832]{2,1,0:T(8,128)(2,1)}, u32[]{:S(2)}, u32[]{:S(2)}) %all-to-all-start.3) | async-done | bytes 4259872 | tf_op jit(solution)/shard_map/all_to_all | solution.py:48
  411.3 6.6 %all-to-all-start.1 = ((bf16[32,80,896]{2,1,0:T(8,128)(2,1)}), bf16[32,80,896]{2,1,0:T(8,128)(2,1)}, u32[]{:S(2)}, u32[]{:S(2)}) async-start(bf16[32,80,896]{2,1,0:T(8,128)(2,1)} %bitcast.11), calls=%async_computation.1 | async-start | bytes 9175040 | tf_op jit(solution)/shard_map/all_to_all | solution.py:48
  417.9 0.0 copy-start
  417.9 0.0 copy-start.1
  417.9 5.5 %convert_reduce_fusion = (f32[80,832]{1,0:T(8,128)S(1)}, f32[80,832]{1,0:T(8,128)S(1)}) fusion(bf16[32,80,832]{2,1,0:T(8,128)(2,1)} %all-to-all-done.3, bf16[32,80,1728]{2,1,0:T(8,128)(2,1)} %param.9), kind=kLoop, calls=%fused_computation.1 | loop fusion | flops 10516480 | bytes 9052160 | tf_op jit(solution)/shard_map/reduce_sum | solution.py:53
  423.4 0.2 divide_subtract_fusion
  423.6 95.9 %all-to-all-done.1 = bf16[32,80,896]{2,1,0:T(8,128)(2,1)} async-done(((bf16[32,80,896]{2,1,0:T(8,128)(2,1)}), bf16[32,80,896]{2,1,0:T(8,128)(2,1)}, u32[]{:S(2)}, u32[]{:S(2)}) %all-to-all-start.1) | async-done | bytes 4587552 | tf_op jit(solution)/shard_map/all_to_all | solution.py:48
  519.5 5.4 %convert_reduce_fusion.1 = (f32[80,896]{1,0:T(8,128)S(1)}, f32[80,896]{1,0:T(8,128)S(1)}) fusion(bf16[32,80,896]{2,1,0:T(8,128)(2,1)} %all-to-all-done.1, bf16[32,80,1728]{2,1,0:T(8,128)(2,1)} %param.9), kind=kLoop, calls=%fused_computation.4 | loop fusion | flops 11325440 | bytes 9748480 | tf_op jit(solution)/shard_map/reduce_sum | solution.py:53
  524.9 0.2 divide_subtract_fusion.1
  525.1 1.1 pad_maximum_fusion
  (7 shorter events, 0.1 us)
Async XLA Ops:
  14.9 10.2 %slice-start = ((f32[80,1728]{1,0:T(8,128)}), f32[80,896]{1,0:T(8,128)S(1)}, s32[]{:S(2)}) async-start(f32[80,1728]{1,0:T(8,128)} %param.7), calls=%async_computation.6 | async-start | bytes 573440 | tf_op jit(solution)/shard_map/slice | solution.py:51
  14.9 111.8 %all-to-all-start.2 = ((bf16[32,80,832]{2,1,0:T(8,128)(2,1)}), bf16[32,80,832]{2,1,0:T(8,128)(2,1)}, u32[]{:S(2)}, u32[]{:S(2)}) async-start(bf16[32,80,832]{2,1,0:T(8,128)(2,1)} %fusion.4), calls=%async_computation.2 | async-start | bytes 9175040 | tf_op jit(solution)/shard_map/all_to_all | solution.py:38
  30.7 102.7 %copy-start.2 = (bf16[64,2560]{1,0:T(8,128)(2,1)S(1)}, bf16[64,2560]{1,0:T(8,128)(2,1)}, u32[]{:S(2)}) copy-start(bf16[64,2560]{1,0:T(8,128)(2,1)} %param.5) | copy-start | bytes 983044
  126.7 174.5 %all-to-all-start = ((bf16[32,80,896]{2,1,0:T(8,128)(2,1)}), bf16[32,80,896]{2,1,0:T(8,128)(2,1)}, u32[]{:S(2)}, u32[]{:S(2)}) async-start(bf16[32,80,896]{2,1,0:T(8,128)(2,1)} %fusion.1), calls=%async_computation | async-start | bytes 9175040 | tf_op jit(solution)/shard_map/all_to_all | solution.py:38
  133.3 81.1 %all-gather.3.cloned.1.call-start = ((), (), s32[]{:S(2)}) async-start(), calls=%async_computation.4 | async-start | bytes 1474560 | tf_op jit(solution)/shard_map/all_gather | solution.py:28
  134.1 149.4 %all-gather.5.cloned.1.call-start = ((), (), s32[]{:S(2)}) async-start(), calls=%async_computation.5 | async-start | bytes 1474560 | tf_op jit(solution)/shard_map/all_gather | solution.py:29
  301.2 110.1 %all-to-all-start.3 = ((bf16[32,80,832]{2,1,0:T(8,128)(2,1)}), bf16[32,80,832]{2,1,0:T(8,128)(2,1)}, u32[]{:S(2)}, u32[]{:S(2)}) async-start(bf16[32,80,832]{2,1,0:T(8,128)(2,1)} %bitcast.10), calls=%async_computation.3 | async-start | bytes 9175040 | tf_op jit(solution)/shard_map/all_to_all | solution.py:48
  411.3 108.3 %all-to-all-start.1 = ((bf16[32,80,896]{2,1,0:T(8,128)(2,1)}), bf16[32,80,896]{2,1,0:T(8,128)(2,1)}, u32[]{:S(2)}, u32[]{:S(2)}) async-start(bf16[32,80,896]{2,1,0:T(8,128)(2,1)} %bitcast.11), calls=%async_computation.1 | async-start | bytes 9175040 | tf_op jit(solution)/shard_map/all_to_all | solution.py:48
  417.9 5.5 %copy-start = (f32[80,1728]{1,0:T(8,128)S(1)}, f32[80,1728]{1,0:T(8,128)}, u32[]{:S(2)}) copy-start(f32[80,1728]{1,0:T(8,128)} %param.8) | copy-start | bytes 1658884
  417.9 5.5 %copy-start.1 = (f32[80,1728]{1,0:T(8,128)S(1)}, f32[80,1728]{1,0:T(8,128)}, u32[]{:S(2)}) copy-start(f32[80,1728]{1,0:T(8,128)} %param.7) | copy-start | bytes 1658884
Sparse Core Ops, SparseCore 0:
  137.3 77.1 all-gather.2
  217.6 65.8 all-gather.4

commit v8 on v5

--- a/solution.py
+++ b/solution.py
@@ -1,7 +1,7 @@
 import jax
 import jax.numpy as jnp
 from jax import lax
-from jax.sharding import PartitionSpec as P
+from jax.sharding import Mesh, PartitionSpec as P
 
 sample_size = 50.0
 weight_decay = 0.02
@@ -23,7 +23,9 @@
 def local(tokens, target, post_mean, post_hess, weight_noise):
     groups = weight_noise.shape[0]
     post_std = lax.rsqrt(sample_size * (post_hess + weight_decay))
-    group_x = lax.all_gather(tokens, "shard", axis=0, tiled=True)
+    pair = lax.all_gather(tokens, "zh", axis=0, tiled=False)
+    quad = lax.all_gather(pair, "y", axis=0, tiled=False)
+    group_x = jnp.swapaxes(quad, 0, 1).reshape(-1, tokens.shape[1])
     chunks = column_chunks(weight_noise.shape[-1])
     my_samples = []
     for lo, hi in chunks:
@@ -68,16 +70,21 @@
 
 
 def solution(mesh):
+    n_shard = mesh.shape["shard"]
+    fine = Mesh(
+        mesh.devices.reshape(mesh.shape["grp"], 2, n_shard // 2), ("grp", "zh", "y")
+    )
+    shard = ("zh", "y")
     return jax.shard_map(
         local,
-        mesh=mesh,
+        mesh=fine,
         in_specs=(
-            P(("grp", "shard"), None),
-            P("grp", "shard"),
-            P("grp", "shard"),
-            P("grp", "shard"),
-            P(None, "grp", "shard"),
+            P(("grp", "zh", "y"), None),
+            P("grp", shard),
+            P("grp", shard),
+            P("grp", shard),
+            P(None, "grp", shard),
         ),
-        out_specs=(P("grp", "shard"), P("grp", "shard")),
+        out_specs=(P("grp", shard), P("grp", shard)),
         check_vma=False,
     )

time: 501 us -> 516 us (1.030)
  blocking collectives: 0 us -> 95.7 us
  waiting for transfers between devices: 395 us -> 312 us
    all_gather x0 -> x1, blocking collectives: none -> 95.7 us  [local(): pair = lax.all_gather(tokens, 'zh', axis=0, tiled=False)]
    all_gather x1, waiting for transfers between devices: 110 us -> 35.5 us  [local(): quad = lax.all_gather(pair, 'y', axis=0, tiled=False)]
    all_to_all x2, waiting for transfers between devices: 103 us -> 96 us  [local(): lax.all_to_all(samples, 'grp', split_axis=0, concat_axis=0, tiled=True)]
  transfers between devices with their start and end apart: 5 -> 5, of which waited for: 5 -> 4; matrix products, arithmetic and copies ran while one was open for 9% -> 9% of each run, Pallas kernels for 0% -> 0%
where the time goes in v8:
time: 516 us; the launch traced here: 515 us
  waiting for transfers between devices  312 us (60%)
  blocking collectives  95.7 us (19%)
  starting transfers between devices  31.7 us (6%)
  other arithmetic  24.7 us (5%)
  matrix products  19.2 us (4%)
  local copies, waits for them, and re-layouts  17.3 us (3%)
  between operations  14.1 us (3%)
    all_to_all x2, waiting for transfers between devices, local(): lax.all_to_all(gradient.reshape(my_sample.shape), 'grp', split_axis=0, co...  181 us
    all_to_all x2, waiting for transfers between devices, local(): lax.all_to_all(samples, 'grp', split_axis=0, concat_axis=0, tiled=True)  96 us
    all_gather x1, blocking collectives, local(): pair = lax.all_gather(tokens, 'zh', axis=0, tiled=False)  95.7 us
    all_gather x1, waiting for transfers between devices, local(): quad = lax.all_gather(pair, 'y', axis=0, tiled=False)  35.5 us
    dot_general x2, matrix products, contract_rows(): lax.dot_general(left, right, (((0,), (0,)), ((), ())), preferred_element_...  19.2 us
    all_to_all x2, starting transfers between devices, local(): lax.all_to_all(samples, 'grp', split_axis=0, concat_axis=0, tiled=True)  16.8 us
    all_to_all x2, starting transfers between devices, local(): lax.all_to_all(gradient.reshape(my_sample.shape), 'grp', split_axis=0, co...  14.9 us
    convert_element_type x2, local copies, waits for them, and re-layouts, local(): gradient = contract_rows(group_x, residual).astype(jnp.bfloat16)  14.3 us
  transfers between devices with their start and end apart: 5, of which 4 were waited for; matrix products, arithmetic and copies ran while one was open for 9% of the time, Pallas kernels for 0%

profile of v8, /device:TPU:1, one launch (start us, length us, event | category | flops | bytes accessed | tf_op | source)
XLA Modules:
  0.0 515.0 jit_solution(14311955549046097191)
XLA Ops:
  7.2 1.0 slice.41
  8.1 1.1 multiply_rsqrt_fusion
  9.3 5.5 %fusion.4 = bf16[32,80,832]{2,1,0:T(8,128)(2,1)} fusion(f32[80,832]{1,0:T(8,128)S(1)} %slice.47, f32[80,832]{1,0:T(8,128)S(1)} %slice.41, bf16[32,80,1728]{2,1,0:T(8,128)(2,1)} %param.9), kind=kLoop, calls=%fused_computation.10 | loop fusion | flops 8519680 | bytes 9052160 | tf_op jit(solution)/shard_map/convert_element_type | solution.py:33
  14.9 10.2 %all-to-all-start.2 = ((bf16[32,80,832]{2,1,0:T(8,128)(2,1)}), bf16[32,80,832]{2,1,0:T(8,128)(2,1)}, u32[]{:S(2)}, u32[]{:S(2)}) async-start(bf16[32,80,832]{2,1,0:T(8,128)(2,1)} %fusion.4), calls=%async_computation.2 | async-start | bytes 9175040 | tf_op jit(solution)/shard_map/all_to_all | solution.py:36
  25.1 0.0 slice-done
  25.1 5.6 %fusion.1 = bf16[32,80,896]{2,1,0:T(8,128)(2,1)} fusion(f32[80,896]{1,0:T(8,128)S(1)} %slice.46, f32[80,896]{1,0:T(8,128)S(1)} %slice-done, bf16[32,80,1728]{2,1,0:T(8,128)(2,1)} %param.9), kind=kLoop, calls=%fused_computation.7 | loop fusion | flops 9175040 | bytes 9748480 | tf_op jit(solution)/shard_map/convert_element_type | solution.py:33
  30.7 96.0 %all-to-all-done.2 = bf16[32,80,832]{2,1,0:T(8,128)(2,1)} async-done(((bf16[32,80,832]{2,1,0:T(8,128)(2,1)}), bf16[32,80,832]{2,1,0:T(8,128)(2,1)}, u32[]{:S(2)}, u32[]{:S(2)}) %all-to-all-start.2) | async-done | bytes 4259872 | tf_op jit(solution)/shard_map/all_to_all | solution.py:36
  126.7 6.6 %all-to-all-start = ((bf16[32,80,896]{2,1,0:T(8,128)(2,1)}), bf16[32,80,896]{2,1,0:T(8,128)(2,1)}, u32[]{:S(2)}, u32[]{:S(2)}) async-start(bf16[32,80,896]{2,1,0:T(8,128)(2,1)} %fusion.1), calls=%async_computation | async-start | bytes 9175040 | tf_op jit(solution)/shard_map/all_to_all | solution.py:36
  133.3 0.0 all-gather.4.cloned.1.call-start
  133.4 0.0 copy-done.2
  133.4 95.7 %all-gather = bf16[128,2560]{1,0:T(8,128)(2,1)} all-gather(bf16[64,2560]{1,0:T(8,128)(2,1)S(1)} %copy-done.2), channel_id=2, replica_groups=mesh['grp'=32,'zh'=2,'y'=4] {'zh'}, dimensions={0}, use_global_device_ids=true | all-gather | bytes 983040 | tf_op jit(solution)/shard_map/all_gather | solution.py:26
  229.1 0.0 all-gather.4.cloned.1.call-update
  229.1 35.5 %all-gather.4.cloned.1.call-done = bf16[8,64,2560]{2,1,0:T(8,128)(2,1)} async-done(((bf16[2,64,2560]{2,1,0:T(8,128)(2,1)}), bf16[8,64,2560]{2,1,0:T(8,128)(2,1)}) %all-gather.4.cloned.1.call-update) | async-done | bytes 2621456 | tf_op jit(solution)/shard_map/all_gather | solution.py:27
  264.7 1.9 copy.14
  266.6 9.6 %fusion.7 = bf16[2560,832]{0,1:T(8,128)(2,1)} fusion(bf16[512,2560]{1,0:T(8,128)(2,1)S(1)} %bitcast.33, bf16[2560,832]{1,0:T(8,128)(2,1)} %bitcast.8, bf16[512,1728]{0,1:T(8,128)(2,1)} %param.6), kind=kOutput, calls=%fused_computation.15 | convolution fusion | flops 4365484032 | bytes 14942208 | tf_op jit(solution)/shard_map/dot_general | solution.py:13
  276.2 7.1 %copy.16 = bf16[2560,832]{1,0:T(8,128)(2,1)} copy(bf16[2560,832]{0,1:T(8,128)(2,1)} %fusion.7) | data formatting | bytes 8519680 | tf_op jit(solution)/shard_map/convert_element_type | solution.py:45
  283.3 0.0 all-to-all-done
  283.3 8.3 %all-to-all-start.3 = ((bf16[32,80,832]{2,1,0:T(8,128)(2,1)}), bf16[32,80,832]{2,1,0:T(8,128)(2,1)}, u32[]{:S(2)}, u32[]{:S(2)}) async-start(bf16[32,80,832]{2,1,0:T(8,128)(2,1)} %bitcast.32), calls=%async_computation.3 | async-start | bytes 9175040 | tf_op jit(solution)/shard_map/all_to_all | solution.py:46
  291.6 9.6 %fusion.6 = bf16[2560,896]{0,1:T(8,128)(2,1)} fusion(bf16[512,2560]{1,0:T(8,128)(2,1)S(1)} %bitcast.34, bf16[2560,896]{1,0:T(8,128)(2,1)} %bitcast, bf16[512,1728]{0,1:T(8,128)(2,1)} %param.6), kind=kOutput, calls=%fused_computation.14 | convolution fusion | flops 4701290496 | bytes 15335424 | tf_op jit(solution)/shard_map/dot_general | solution.py:13
  301.2 7.2 %copy.15 = bf16[2560,896]{1,0:T(8,128)(2,1)} copy(bf16[2560,896]{0,1:T(8,128)(2,1)} %fusion.6) | data formatting | bytes 9175040 | tf_op jit(solution)/shard_map/convert_element_type | solution.py:45
  308.4 84.8 %all-to-all-done.3 = bf16[32,80,832]{2,1,0:T(8,128)(2,1)} async-done(((bf16[32,80,832]{2,1,0:T(8,128)(2,1)}), bf16[32,80,832]{2,1,0:T(8,128)(2,1)}, u32[]{:S(2)}, u32[]{:S(2)}) %all-to-all-start.3) | async-done | bytes 4259872 | tf_op jit(solution)/shard_map/all_to_all | solution.py:46
  393.2 6.6 %all-to-all-start.1 = ((bf16[32,80,896]{2,1,0:T(8,128)(2,1)}), bf16[32,80,896]{2,1,0:T(8,128)(2,1)}, u32[]{:S(2)}, u32[]{:S(2)}) async-start(bf16[32,80,896]{2,1,0:T(8,128)(2,1)} %bitcast.31), calls=%async_computation.1 | async-start | bytes 9175040 | tf_op jit(solution)/shard_map/all_to_all | solution.py:46
  399.8 0.0 copy-start
  399.8 0.0 copy-start.1
  399.8 5.5 %convert_reduce_fusion = (f32[80,832]{1,0:T(8,128)S(1)}, f32[80,832]{1,0:T(8,128)S(1)}) fusion(bf16[32,80,832]{2,1,0:T(8,128)(2,1)} %all-to-all-done.3, bf16[32,80,1728]{2,1,0:T(8,128)(2,1)} %param.9), kind=kLoop, calls=%fused_computation.1 | loop fusion | flops 10516480 | bytes 9052160 | tf_op jit(solution)/shard_map/reduce_sum | solution.py:51
  405.3 0.0 copy-done
  405.4 0.0 copy-done.1
  405.4 0.2 divide_subtract_fusion
  405.6 95.9 %all-to-all-done.1 = bf16[32,80,896]{2,1,0:T(8,128)(2,1)} async-done(((bf16[32,80,896]{2,1,0:T(8,128)(2,1)}), bf16[32,80,896]{2,1,0:T(8,128)(2,1)}, u32[]{:S(2)}, u32[]{:S(2)}) %all-to-all-start.1) | async-done | bytes 4587552 | tf_op jit(solution)/shard_map/all_to_all | solution.py:46
  501.5 5.4 %convert_reduce_fusion.1 = (f32[80,896]{1,0:T(8,128)S(1)}, f32[80,896]{1,0:T(8,128)S(1)}) fusion(bf16[32,80,896]{2,1,0:T(8,128)(2,1)} %all-to-all-done.1, bf16[32,80,1728]{2,1,0:T(8,128)(2,1)} %param.9), kind=kLoop, calls=%fused_computation.4 | loop fusion | flops 11325440 | bytes 9748480 | tf_op jit(solution)/shard_map/reduce_sum | solution.py:51
  506.8 0.2 divide_subtract_fusion.1
  507.1 1.1 pad_maximum_fusion
  (4 shorter events, 0.0 us)
Async XLA Ops:
  14.9 10.2 %slice-start = ((f32[80,1728]{1,0:T(8,128)}), f32[80,896]{1,0:T(8,128)S(1)}, s32[]{:S(2)}) async-start(f32[80,1728]{1,0:T(8,128)} %param.7), calls=%async_computation.5 | async-start | bytes 573440 | tf_op jit(solution)/shard_map/slice | solution.py:49
  14.9 111.8 %all-to-all-start.2 = ((bf16[32,80,832]{2,1,0:T(8,128)(2,1)}), bf16[32,80,832]{2,1,0:T(8,128)(2,1)}, u32[]{:S(2)}, u32[]{:S(2)}) async-start(bf16[32,80,832]{2,1,0:T(8,128)(2,1)} %fusion.4), calls=%async_computation.2 | async-start | bytes 9175040 | tf_op jit(solution)/shard_map/all_to_all | solution.py:36
  30.7 102.7 %copy-start.2 = (bf16[64,2560]{1,0:T(8,128)(2,1)S(1)}, bf16[64,2560]{1,0:T(8,128)(2,1)}, u32[]{:S(2)}) copy-start(bf16[64,2560]{1,0:T(8,128)(2,1)} %param.5) | copy-start | bytes 983044
  126.7 156.6 %all-to-all-start = ((bf16[32,80,896]{2,1,0:T(8,128)(2,1)}), bf16[32,80,896]{2,1,0:T(8,128)(2,1)}, u32[]{:S(2)}, u32[]{:S(2)}) async-start(bf16[32,80,896]{2,1,0:T(8,128)(2,1)} %fusion.1), calls=%async_computation | async-start | bytes 9175040 | tf_op jit(solution)/shard_map/all_to_all | solution.py:36
  133.3 131.4 %all-gather.4.cloned.1.call-start = ((), (), s32[]{:S(2)}) async-start(), calls=%async_computation.4 | async-start | bytes 3276800 | tf_op jit(solution)/shard_map/all_gather | solution.py:27
  283.3 109.9 %all-to-all-start.3 = ((bf16[32,80,832]{2,1,0:T(8,128)(2,1)}), bf16[32,80,832]{2,1,0:T(8,128)(2,1)}, u32[]{:S(2)}, u32[]{:S(2)}) async-start(bf16[32,80,832]{2,1,0:T(8,128)(2,1)} %bitcast.32), calls=%async_computation.3 | async-start | bytes 9175040 | tf_op jit(solution)/shard_map/all_to_all | solution.py:46
  393.2 108.3 %all-to-all-start.1 = ((bf16[32,80,896]{2,1,0:T(8,128)(2,1)}), bf16[32,80,896]{2,1,0:T(8,128)(2,1)}, u32[]{:S(2)}, u32[]{:S(2)}) async-start(bf16[32,80,896]{2,1,0:T(8,128)(2,1)} %bitcast.31), calls=%async_computation.1 | async-start | bytes 9175040 | tf_op jit(solution)/shard_map/all_to_all | solution.py:46
  399.8 5.5 %copy-start = (f32[80,1728]{1,0:T(8,128)S(1)}, f32[80,1728]{1,0:T(8,128)}, u32[]{:S(2)}) copy-start(f32[80,1728]{1,0:T(8,128)} %param.8) | copy-start | bytes 1658884
  399.8 5.5 %copy-start.1 = (f32[80,1728]{1,0:T(8,128)S(1)}, f32[80,1728]{1,0:T(8,128)}, u32[]{:S(2)}) copy-start(f32[80,1728]{1,0:T(8,128)} %param.7) | copy-start | bytes 1658884
Sparse Core Ops, SparseCore 0:
  229.3 35.3 all-gather.3
